TPU v7x, 32 devices: a whole 2x2x4 slice. The times are simulated.
32 devices in a mesh: dp: 8 (over z, y), tensor: 4 (over x, core).
Axes of the slice: x: 2, y: 2, z: 4, core: 2. Of those that a mesh axis runs over, the one named last changes fastest.
Arguments:
- inputs: bfloat16 [16, 1024, 512], P('dp', 'tensor'), may hold values from -6 to 6
- memory: bfloat16 [16, 1024, 512], P('dp', 'tensor'), may hold values from -6 to 6
- tgt_len: int32 [16], P('dp'), may hold values from 512 to 1024, as said below
- src_len: int32 [16], P('dp'), may hold values from 512 to 1024, as said below
- cotangent: bfloat16 [16, 1024, 512], P('dp', 'tensor'), may hold values from -6 to 6
- w_qkv: bfloat16 [3, 512, 512], P(None, 'dp', 'tensor'), may hold values from -0.25 to 0.25
- w_out: bfloat16 [512, 512], P('tensor', 'dp'), may hold values from -6 to 6
- cross_query: bfloat16 [512, 512], P('dp', 'tensor'), may hold values from -0.25 to 0.25
- cross_kv: bfloat16 [2, 512, 512], P(None, 'dp', 'tensor'), may hold values from -0.25 to 0.25
- cross_out: bfloat16 [512, 512], P('tensor', 'dp'), may hold values from -6 to 6
- ffn_up: bfloat16 [512, 2048], P('dp', 'tensor'), may hold values from -0.25 to 0.25
- ffn_down: bfloat16 [2048, 512], P('tensor', 'dp'), may hold values from -0.1875 to 0.1875
- gain_one: bfloat16 [512], P('dp'), may hold values from 0.099609375 to 1.8984375
- bias_one: bfloat16 [512], P('dp'), may hold values from -3 to 3
- gain_two: bfloat16 [512], P('dp'), may hold values from 0.099609375 to 1.8984375
- bias_two: bfloat16 [512], P('dp'), may hold values from -3 to 3
- gain_three: bfloat16 [512], P('dp'), may hold values from 0.099609375 to 1.8984375
- bias_three: bfloat16 [512], P('dp'), may hold values from -3 to 3
Outputs:
- output: bfloat16 [16, 1024, 512], P('dp', 'tensor')
- grad_inputs: float32 [16, 1024, 512], P('dp', 'tensor')
- grad_memory: float32 [16, 1024, 512], P('dp', 'tensor')
- grad_w_qkv: float32 [3, 512, 512], P(None, 'dp', 'tensor')
- grad_w_out: float32 [512, 512], P('tensor', 'dp')
- grad_cross_query: float32 [512, 512], P('dp', 'tensor')
- grad_cross_kv: float32 [2, 512, 512], P(None, 'dp', 'tensor')
- grad_cross_out: float32 [512, 512], P('tensor', 'dp')
- grad_ffn_up: float32 [512, 2048], P('dp', 'tensor')
- grad_ffn_down: float32 [2048, 512], P('tensor', 'dp')
- grad_gain_one: float32 [512], P('dp')
- grad_bias_one: float32 [512], P('dp')
- grad_gain_two: float32 [512], P('dp')
- grad_bias_two: float32 [512], P('dp')
- grad_gain_three: float32 [512], P('dp')
- grad_bias_three: float32 [512], P('dp')
Inputs may be any that keep to these rules, and one draw needn't show every extreme that they name: `tgt_len`: one sequence has a target length of 1024 and another of 512. `src_len`: one sequence has a source length of 1024 and another of 512.
All inputs are finite; a program needn't handle non-finite values.
Results may differ from a plain program's by a relative error of at most 0.015.
Values may be sent and summed in bfloat16 or wider, within the bound.
A program may use at most 128 MiB of HBM per device.

v0:
```python
import jax
import jax.numpy as jnp
from jax import lax
from jax.sharding import PartitionSpec as P

DH = 64
EPSILON = 1e-05
MASKED = -1e30
BLOCK_ROWS = 512


def layer_norm(values, gain_vec, bias_vec):
    center = values - jnp.mean(values, axis=-1, keepdims=True)
    spread = jnp.mean(center * center, axis=-1, keepdims=True)
    return center * lax.rsqrt(spread + EPSILON) * gain_vec + bias_vec


def smooth_gate(values):
    return jax.nn.gelu(values, approximate=True)


def gather_weights(
    w_qkv,
    w_out,
    cross_query,
    cross_kv,
    cross_out,
    ffn_up,
    ffn_down,
    gain_one,
    bias_one,
    gain_two,
    bias_two,
    gain_three,
    bias_three,
):
    return (
        lax.all_gather(w_qkv, "dp", axis=1, tiled=True),
        lax.all_gather(w_out, "dp", axis=1, tiled=True),
        lax.all_gather(cross_query, "dp", axis=0, tiled=True),
        lax.all_gather(cross_kv, "dp", axis=1, tiled=True),
        lax.all_gather(cross_out, "dp", axis=1, tiled=True),
        lax.all_gather(ffn_up, "dp", axis=0, tiled=True),
        lax.all_gather(ffn_down, "dp", axis=1, tiled=True),
        lax.all_gather(gain_one, "dp", axis=0, tiled=True),
        lax.all_gather(bias_one, "dp", axis=0, tiled=True),
        lax.all_gather(gain_two, "dp", axis=0, tiled=True),
        lax.all_gather(bias_two, "dp", axis=0, tiled=True),
        lax.all_gather(gain_three, "dp", axis=0, tiled=True),
        lax.all_gather(bias_three, "dp", axis=0, tiled=True),
    )


def reduce_grads(
    grad_qkv,
    grad_out,
    grad_query,
    grad_pair,
    grad_cross,
    grad_up,
    grad_down,
    grad_gain_one,
    grad_bias_one,
    grad_gain_two,
    grad_bias_two,
    grad_gain_three,
    grad_bias_three,
):
    return (
        lax.psum_scatter(grad_qkv, "dp", scatter_dimension=1, tiled=True),
        lax.psum_scatter(grad_out, "dp", scatter_dimension=1, tiled=True),
        lax.psum_scatter(grad_query, "dp", scatter_dimension=0, tiled=True),
        lax.psum_scatter(grad_pair, "dp", scatter_dimension=1, tiled=True),
        lax.psum_scatter(grad_cross, "dp", scatter_dimension=1, tiled=True),
        lax.psum_scatter(grad_up, "dp", scatter_dimension=0, tiled=True),
        lax.psum_scatter(grad_down, "dp", scatter_dimension=1, tiled=True),
        lax.psum_scatter(grad_gain_one, "dp", scatter_dimension=0, tiled=True),
        lax.psum_scatter(grad_bias_one, "dp", scatter_dimension=0, tiled=True),
        lax.psum_scatter(grad_gain_two, "dp", scatter_dimension=0, tiled=True),
        lax.psum_scatter(grad_bias_two, "dp", scatter_dimension=0, tiled=True),
        lax.psum_scatter(grad_gain_three, "dp", scatter_dimension=0, tiled=True),
        lax.psum_scatter(grad_bias_three, "dp", scatter_dimension=0, tiled=True),
    )


def norm_rows(own_part):
    return lax.all_gather(own_part, "tensor", axis=0, tiled=True)


def grad_rows(own_part):
    return lax.all_gather(own_part, "tensor", axis=0, tiled=True)


def branch_sum(mixture, weight):
    return lax.psum_scatter(
        jnp.dot(mixture, weight, preferred_element_type=jnp.float32),
        "tensor",
        scatter_dimension=0,
        tiled=True,
    )


def input_grad(grad_term, own_rows):
    return lax.psum_scatter(
        grad_term(jnp.int32(0), own_rows * lax.axis_size("tensor")),
        "tensor",
        scatter_dimension=0,
        tiled=True,
    )


def head_view(matrix):
    return matrix.reshape(matrix.shape[0], -1, DH)


def block_scores(query_block, key_heads, first_row, causal, length):
    scores = jnp.einsum("qhd,khd->hqk", query_block, key_heads, preferred_element_type=jnp.float32)
    scores = scores * DH ** (-0.5)
    row_ids = first_row + jnp.arange(query_block.shape[0])
    col_ids = jnp.arange(key_heads.shape[0])
    live_mask = col_ids[None, :] < length
    if causal:
        live_mask = live_mask & (col_ids[None, :] <= row_ids[:, None])
    return jnp.where(live_mask[None], scores, MASKED)


def attend_forward(queries, key_rows, value_rows, causal, length):
    row_total = queries.shape[0]
    block_size = min(BLOCK_ROWS, row_total)
    blocks = row_total // block_size
    query_heads = head_view(queries).reshape(blocks, block_size, -1, DH)
    key_heads = head_view(key_rows)
    value_heads = head_view(value_rows)

    def one_block(members):
        query_block, block_index = members
        scores = block_scores(query_block, key_heads, block_index * block_size, causal, length)
        row_max = jnp.max(scores, axis=-1, keepdims=True)
        shifted = jnp.exp(scores - row_max)
        summed = jnp.sum(shifted, axis=-1, keepdims=True)
        weights = (shifted / summed).astype(jnp.bfloat16)
        mixture = jnp.einsum(
            "hqk,khd->qhd", weights, value_heads, preferred_element_type=jnp.float32
        )
        return (mixture.astype(jnp.bfloat16), (row_max + jnp.log(summed))[..., 0])

    mixture, log_norm = lax.map(one_block, (query_heads, jnp.arange(blocks)))
    return (mixture.reshape(row_total, -1), log_norm)


def attend_backward(queries, key_rows, value_rows, grad_mix, log_norm, causal, length):
    row_total = queries.shape[0]
    block_size = min(BLOCK_ROWS, row_total)
    blocks = row_total // block_size
    query_heads = head_view(queries).reshape(blocks, block_size, -1, DH)
    grad_heads = head_view(grad_mix).reshape(blocks, block_size, -1, DH)
    key_heads = head_view(key_rows)
    value_heads = head_view(value_rows)
    scale_value = DH ** (-0.5)

    def one_block(carry, members):
        query_block, grad_block, norm_block, block_index = members
        scores = block_scores(query_block, key_heads, block_index * block_size, causal, length)
        probs = jnp.exp(scores - norm_block[..., None])
        grad_probs = jnp.einsum(
            "qhd,khd->hqk", grad_block, value_heads, preferred_element_type=jnp.float32
        )
        inner = jnp.sum(probs * grad_probs, axis=-1, keepdims=True)
        grad_scores = (probs * (grad_probs - inner)).astype(jnp.bfloat16)
        grad_query = (
            jnp.einsum("hqk,khd->qhd", grad_scores, key_heads, preferred_element_type=jnp.float32)
            * scale_value
        )
        key_sum, value_sum = carry
        key_sum = (
            key_sum
            + jnp.einsum(
                "hqk,qhd->khd", grad_scores, query_block, preferred_element_type=jnp.float32
            )
            * scale_value
        )
        value_sum = value_sum + jnp.einsum(
            "hqk,qhd->khd",
            probs.astype(jnp.bfloat16),
            grad_block,
            preferred_element_type=jnp.float32,
        )
        return ((key_sum, value_sum), grad_query)

    zeros = jnp.zeros(key_heads.shape, jnp.float32)
    (key_sum, value_sum), grad_query = lax.scan(
        one_block, (zeros, zeros), (query_heads, grad_heads, log_norm, jnp.arange(blocks))
    )
    key_total = key_rows.shape[0]
    return (
        grad_query.reshape(row_total, -1),
        key_sum.reshape(key_total, -1),
        value_sum.reshape(key_total, -1),
    )


def widened(shard, dim, factor):
    shape_list = list(shard.shape)
    shape_list[dim] = shape_list[dim] * factor
    return jnp.zeros(shape_list, jnp.float32)


def body(
    inputs,
    memory,
    tgt_len,
    src_len,
    cotangent,
    w_qkv,
    w_out,
    cross_query,
    cross_kv,
    cross_out,
    ffn_up,
    ffn_down,
    gain_one,
    bias_one,
    gain_two,
    bias_two,
    gain_three,
    bias_three,
):
    own_rows = inputs.shape[1]
    row_first = lax.axis_index("tensor") * own_rows
    shards = (
        w_qkv,
        w_out,
        cross_query,
        cross_kv,
        cross_out,
        ffn_up,
        ffn_down,
        gain_one,
        bias_one,
        gain_two,
        bias_two,
        gain_three,
        bias_three,
    )
    shard_dims = (1, 1, 0, 1, 1, 0, 1, 0, 0, 0, 0, 0, 0)
    dp_count = lax.axis_size("dp")
    accum_list = [
        widened(shard, dim_index, dp_count) for shard, dim_index in zip(shards, shard_dims)
    ]
    accum_init = tuple(accum_list)

    def advance(accum, members):
        own_in, own_memory, tgt_count, src_count, own_cot = members
        gathered = gather_weights(*shards)
        live_rows = (row_first + jnp.arange(own_rows) < tgt_count).astype(jnp.float32)[:, None]
        residual_in = own_in.astype(jnp.float32)
        normed, pull_one = jax.vjp(
            layer_norm,
            residual_in,
            gathered[7].astype(jnp.float32),
            gathered[8].astype(jnp.float32),
        )
        normed_all = norm_rows(normed.astype(jnp.bfloat16))
        projected = jnp.einsum(
            "td,jdh->jth", normed_all, gathered[0], preferred_element_type=jnp.float32
        ).astype(jnp.bfloat16)
        self_mix, self_norm = attend_forward(
            projected[0], projected[1], projected[2], True, tgt_count
        )
        hidden_one = residual_in + branch_sum(self_mix, gathered[1])
        normed, pull_two = jax.vjp(
            layer_norm,
            hidden_one,
            gathered[9].astype(jnp.float32),
            gathered[10].astype(jnp.float32),
        )
        cross_all, memory_all = (
            lax.all_gather(normed.astype(jnp.bfloat16), "tensor", axis=0, tiled=True),
            lax.all_gather(own_memory, "tensor", axis=0, tiled=True),
        )
        cross_queries = jnp.dot(cross_all, gathered[2], preferred_element_type=jnp.float32).astype(
            jnp.bfloat16
        )
        cross_pair = jnp.einsum(
            "sd,jdh->jsh", memory_all, gathered[3], preferred_element_type=jnp.float32
        ).astype(jnp.bfloat16)
        cross_mix, cross_norm = attend_forward(
            cross_queries, cross_pair[0], cross_pair[1], False, src_count
        )
        hidden_two = hidden_one + branch_sum(cross_mix, gathered[4])
        normed, pull_three = jax.vjp(
            layer_norm,
            hidden_two,
            gathered[11].astype(jnp.float32),
            gathered[12].astype(jnp.float32),
        )
        grad_out = live_rows * own_cot.astype(jnp.float32)
        ffn_rows = norm_rows(normed.astype(jnp.bfloat16))
        before = jnp.dot(ffn_rows, gathered[5], preferred_element_type=jnp.float32)
        gated, gate_pull = jax.vjp(smooth_gate, before)
        active = gated.astype(jnp.bfloat16)
        output = live_rows * (hidden_two + branch_sum(active, gathered[6]))
        grad_all = grad_rows(grad_out.astype(jnp.bfloat16))
        grad_down = jnp.einsum("tf,td->fd", active, grad_all, preferred_element_type=jnp.float32)
        grad_active = jnp.einsum(
            "td,fd->tf", grad_all, gathered[6], preferred_element_type=jnp.float32
        )
        grad_before = gate_pull(grad_active)[0].astype(jnp.bfloat16)
        grad_up = jnp.einsum("td,tf->df", ffn_rows, grad_before, preferred_element_type=jnp.float32)

        def ffn_term(first_row, row_count):
            return jnp.einsum(
                "tf,df->td", grad_before, gathered[5], preferred_element_type=jnp.float32
            )

        back_three = input_grad(ffn_term, own_rows)
        grad_hidden, grad_gain_three, grad_bias_three = pull_three(back_three)
        grad_two = grad_out + grad_hidden
        grad_all = grad_rows(grad_two.astype(jnp.bfloat16))
        grad_cross = jnp.einsum(
            "th,td->hd", cross_mix, grad_all, preferred_element_type=jnp.float32
        )
        grad_mix = jnp.einsum(
            "td,hd->th", grad_all, gathered[4], preferred_element_type=jnp.float32
        ).astype(jnp.bfloat16)
        grad_cq, grad_ck, grad_cv = attend_backward(
            cross_queries, cross_pair[0], cross_pair[1], grad_mix, cross_norm, False, src_count
        )
        grad_cq = grad_cq.astype(jnp.bfloat16)
        grad_ckv = jnp.stack([grad_ck, grad_cv]).astype(jnp.bfloat16)
        grad_query = jnp.einsum("td,th->dh", cross_all, grad_cq, preferred_element_type=jnp.float32)
        grad_pair = jnp.einsum(
            "sd,jsh->jdh", memory_all, grad_ckv, preferred_element_type=jnp.float32
        )
        back_rows = jnp.einsum(
            "th,dh->td", grad_cq, gathered[2], preferred_element_type=jnp.float32
        )
        back_memory = jnp.einsum(
            "jsh,jdh->sd", grad_ckv, gathered[3], preferred_element_type=jnp.float32
        )
        own_back, grad_encoded = (
            lax.psum_scatter(back_rows, "tensor", scatter_dimension=0, tiled=True),
            lax.psum_scatter(back_memory, "tensor", scatter_dimension=0, tiled=True),
        )
        grad_hidden, grad_gain_two, grad_bias_two = pull_two(own_back)
        grad_one = grad_two + grad_hidden
        grad_all = grad_rows(grad_one.astype(jnp.bfloat16))
        grad_self_out = jnp.einsum(
            "th,td->hd", self_mix, grad_all, preferred_element_type=jnp.float32
        )
        grad_mix = jnp.einsum(
            "td,hd->th", grad_all, gathered[1], preferred_element_type=jnp.float32
        ).astype(jnp.bfloat16)
        grad_sq, grad_sk, grad_sv = attend_backward(
            projected[0], projected[1], projected[2], grad_mix, self_norm, True, tgt_count
        )
        grad_triple = jnp.stack([grad_sq, grad_sk, grad_sv]).astype(jnp.bfloat16)
        grad_qkv = jnp.einsum(
            "td,jth->jdh", normed_all, grad_triple, preferred_element_type=jnp.float32
        )

        def self_term(first_row, row_count):
            return jnp.einsum(
                "jth,jdh->td", grad_triple, gathered[0], preferred_element_type=jnp.float32
            )

        grad_hidden, grad_gain_one, grad_bias_one = pull_one(input_grad(self_term, own_rows))
        grad_values = grad_one + grad_hidden
        grads = (
            grad_qkv,
            grad_self_out,
            grad_query,
            grad_pair,
            grad_cross,
            grad_up,
            grad_down,
            grad_gain_one,
            grad_bias_one,
            grad_gain_two,
            grad_bias_two,
            grad_gain_three,
            grad_bias_three,
        )
        accum = jax.tree.map(jnp.add, accum, grads)
        return (accum, (output.astype(jnp.bfloat16), grad_values, grad_encoded))

    accum, (outputs, grad_inputs, grad_memory) = lax.scan(
        advance, accum_init, (inputs, memory, tgt_len, src_len, cotangent)
    )
    accum_list = list(accum)
    accum = reduce_grads(*accum_list)
    norm_grads = lax.psum((accum[7], accum[8], accum[9], accum[10], accum[11], accum[12]), "tensor")
    return (
        outputs,
        grad_inputs,
        grad_memory,
        accum[0],
        accum[1],
        accum[2],
        accum[3],
        accum[4],
        accum[5],
        accum[6],
        norm_grads[0],
        norm_grads[1],
        norm_grads[2],
        norm_grads[3],
        norm_grads[4],
        norm_grads[5],
    )


def solution(mesh):
    return jax.shard_map(
        body,
        mesh=mesh,
        in_specs=(
            P("dp", "tensor", None),
            P("dp", "tensor", None),
            P("dp"),
            P("dp"),
            P("dp", "tensor", None),
            P(None, "dp", "tensor"),
            P("tensor", "dp"),
            P("dp", "tensor"),
            P(None, "dp", "tensor"),
            P("tensor", "dp"),
            P("dp", "tensor"),
            P("tensor", "dp"),
            P("dp"),
            P("dp"),
            P("dp"),
            P("dp"),
            P("dp"),
            P("dp"),
        ),
        out_specs=(
            P("dp", "tensor", None),
            P("dp", "tensor", None),
            P("dp", "tensor", None),
            P(None, "dp", "tensor"),
            P("tensor", "dp"),
            P("dp", "tensor"),
            P(None, "dp", "tensor"),
            P("tensor", "dp"),
            P("dp", "tensor"),
            P("tensor", "dp"),
            P("dp"),
            P("dp"),
            P("dp"),
            P("dp"),
            P("dp"),
            P("dp"),
        ),
        check_vma=False,
    )
```

profile of v0, /device:TPU:0, one launch (start us, length us, event | category | flops | bytes accessed | tf_op | source)
XLA Modules:
  0.0 1706.3 jit_solution(2830867907719155688)
XLA Ops:
  8.2 1231.4 %while.159 = (s32[]{:T(128)}, f32[3,512,128]{1,2,0:T(8,128)}, f32[128,512]{1,0:T(8,128)}, f32[512,128]{1,0:T(8,128)}, f32[2,512,128]{1,2,0:T(8,128)}, /*index=5*...) while((s32[]{:T(128)}, f32[3,512,128]{1,2,0:T(8,128)}, ...), condition=%wide.region_40.41_spmd.clone, body=%wide.region_0.40_spmd.clone.sunk | while | flops 8421522944 | bytes 381262368 | solution.py:387
  41.5 23.9 %all-reduce.22 = (bf16[512]{0:T(512)(128)(2,1)S(1)}, bf16[512]{0:T(512)(128)(2,1)S(1)}, bf16[512]{0:T(512)(128)(2,1)S(1)}, bf16[512]{0:T(512)(128)(2,1)S(1)}, bf...) all-reduce(bf16[512]{0:T(512)(128)(2,1)S(1)} %dynamic-update-slice.18, ...), channel_id=1, replica_groups=mesh['dp'=8,'tensor'=4] {'dp'}, use_global_device_ids=true, to_apply=%add.1 | all-reduce | flops 3072 | bytes 12288 | tf_op jit(solution)/shard_map/while
  68.6 30.7 %all_gather.148 = bf16[128,512]{0,1:T(8,128)(2,1)S(1)} all-gather(bf16[128,64]{0,1:T(8,128)(2,1)} %get-tuple-element.2082), channel_id=1, replica_groups=mesh['dp'=8,'tensor'=4] {'dp'}, dimensions={1}, use_global_device_ids=true | all-gather | bytes 147456 | tf_op jit(solution)/shard_map/while/body/eval_jaxpr/all_gather | solution.py:39
  99.3 31.2 %all_gather.147 = bf16[3,512,128]{2,1,0:T(8,128)(2,1)S(1)} all-gather(bf16[3,64,128]{2,1,0:T(8,128)(2,1)} %get-tuple-element.2077), channel_id=1, replica_groups=mesh['dp'=8,'tensor'=4] {'dp'}, dimensions={1}, use_global_device_ids=true | all-gather | bytes 442368 | tf_op jit(solution)/shard_map/while/body/eval_jaxpr/all_gather | solution.py:38
  133.4 12.2 while.160
  149.5 27.9 %reduce-scatter.29.cloned.1.call-done = f32[256,512]{1,0:T(8,128)} async-done(((f32[1024,512]{1,0:T(8,128)}), f32[256,512]{1,0:T(8,128)}) %reduce-scatter.29.cloned.1.call-update) | async-done | bytes 524304 | tf_op jit(solution)/shard_map/while/body/eval_jaxpr/reduce_scatter | solution.py:95
  180.4 30.6 %all_gather.154 = bf16[128,512]{0,1:T(8,128)(2,1)S(1)} all-gather(bf16[128,64]{0,1:T(8,128)(2,1)S(1)} %copy-done.65), channel_id=1, replica_groups=mesh['dp'=8,'tensor'=4] {'dp'}, dimensions={1}, use_global_device_ids=true | all-gather | bytes 147456 | tf_op jit(solution)/shard_map/while/body/eval_jaxpr/all_gather | solution.py:42
  210.9 30.5 %all_gather.150 = bf16[512,128]{1,0:T(8,128)(2,1)S(1)} all-gather(bf16[64,128]{1,0:T(8,128)(2,1)S(1)} %copy-done.64), channel_id=1, replica_groups=mesh['dp'=8,'tensor'=4] {'dp'}, dimensions={0}, use_global_device_ids=true | all-gather | bytes 147456 | tf_op jit(solution)/shard_map/while/body/eval_jaxpr/all_gather | solution.py:40
  241.4 30.7 %all_gather.151 = bf16[2,512,128]{2,1,0:T(8,128)(2,1)S(1)} all-gather(bf16[2,64,128]{2,1,0:T(8,128)(2,1)S(1)} %copy-done.50), channel_id=1, replica_groups=mesh['dp'=8,'tensor'=4] {'dp'}, dimensions={1}, use_global_device_ids=true | all-gather | bytes 294912 | tf_op jit(solution)/shard_map/while/body/eval_jaxpr/all_gather | solution.py:41
  276.5 8.1 while.161
  290.4 28.5 %reduce-scatter.31.cloned.1.call-done = f32[256,512]{1,0:T(8,128)} async-done(((f32[1024,512]{1,0:T(8,128)}), f32[256,512]{1,0:T(8,128)}) %reduce-scatter.31.cloned.1.call-update) | async-done | bytes 524304 | tf_op jit(solution)/shard_map/while/body/eval_jaxpr/reduce_scatter | solution.py:95
  321.3 33.6 %all_gather.156 = bf16[512,512]{1,0:T(8,128)(2,1)} all-gather(bf16[64,512]{1,0:T(8,128)(2,1)S(1)} %copy-done.38), channel_id=1, replica_groups=mesh['dp'=8,'tensor'=4] {'dp'}, dimensions={0}, use_global_device_ids=true | all-gather | bytes 589824 | tf_op jit(solution)/shard_map/while/body/eval_jaxpr/all_gather | solution.py:43
  355.0 31.2 %all_gather.153 = bf16[512,512]{0,1:T(8,128)(2,1)S(1)} all-gather(bf16[512,64]{0,1:T(8,128)(2,1)S(1)} %copy-done.37), channel_id=1, replica_groups=mesh['dp'=8,'tensor'=4] {'dp'}, dimensions={1}, use_global_device_ids=true | all-gather | bytes 589824 | tf_op jit(solution)/shard_map/while/body/eval_jaxpr/all_gather | solution.py:44
  386.2 3.5 fusion.336
  389.7 5.3 fusion.340
  398.1 31.7 %reduce-scatter.33.cloned.1.call-done = f32[256,512]{1,0:T(8,128)} async-done(((f32[1024,512]{1,0:T(8,128)}), f32[256,512]{1,0:T(8,128)}) %reduce-scatter.33.cloned.1.call-update) | async-done | bytes 524304 | tf_op jit(solution)/shard_map/while/body/eval_jaxpr/reduce_scatter | solution.py:104
  434.7 16.8 all-gather.22.cloned.1.call-done
  457.9 13.5 while.162
  472.8 2.8 fusion.344
  475.6 31.5 %reduce-scatter.35.cloned.1.call-done = f32[256,512]{1,0:T(8,128)} async-done(((f32[1024,512]{1,0:T(8,128)}), f32[256,512]{1,0:T(8,128)}) %reduce-scatter.35.cloned.1.call-update) | async-done | bytes 524304 | tf_op jit(solution)/shard_map/while/body/eval_jaxpr/reduce_scatter | solution.py:342
  512.5 3.9 fusion.351
  520.3 9.0 all-gather.24.cloned.1.call-done
  532.4 21.7 %while.163 = (s32[]{:T(128)}, f32[1024,2,64]{0,2,1:T(8,128)S(1)}, f32[1024,2,64]{0,2,1:T(8,128)}, bf16[2,512,2,64]{1,3,2,0:T(8,128)(2,1)}, bf16[2,512,2,64]{1,3,...) while((s32[]{:T(128)}, f32[1024,2,64]{0,2,1:T(8,128)S(1)}, ...), condition=%wide.region_28.28_spmd.clone, body=%wide.region_26.27_spmd.clone.sunk | while | flops 688587264 | bytes 37259468 | solution.py:191
  545.8 3.2 fusion.389
  559.8 3.1 convolution_add_fusion.13
  573.1 24.2 %reduce-scatter.41.cloned.1.call-done = f32[256,512]{1,0:T(8,128)} async-done(((f32[1024,512]{1,0:T(8,128)}), f32[256,512]{1,0:T(8,128)}) %reduce-scatter.41.cloned.1.call-update) | async-done | bytes 524304 | tf_op jit(solution)/shard_map/while/body/eval_jaxpr/reduce_scatter | solution.py:343
  601.6 2.9 fusion.347
  604.5 26.7 %reduce-scatter.37.cloned.1.call-done = f32[256,512]{1,0:T(8,128)} async-done(((f32[1024,512]{1,0:T(8,128)}), f32[256,512]{1,0:T(8,128)}) %reduce-scatter.37.cloned.1.call-update) | async-done | bytes 524304 | tf_op jit(solution)/shard_map/while/body/eval_jaxpr/reduce_scatter | solution.py:104
  645.6 22.1 %all-reduce.22 = (bf16[512]{0:T(512)(128)(2,1)S(1)}, bf16[512]{0:T(512)(128)(2,1)S(1)}, bf16[512]{0:T(512)(128)(2,1)S(1)}, bf16[512]{0:T(512)(128)(2,1)S(1)}, bf...) all-reduce(bf16[512]{0:T(512)(128)(2,1)S(1)} %dynamic-update-slice.18, ...), channel_id=1, replica_groups=mesh['dp'=8,'tensor'=4] {'dp'}, use_global_device_ids=true, to_apply=%add.1 | all-reduce | flops 3072 | bytes 12288 | tf_op jit(solution)/shard_map/while
  670.9 30.7 %all_gather.148 = bf16[128,512]{0,1:T(8,128)(2,1)S(1)} all-gather(bf16[128,64]{0,1:T(8,128)(2,1)} %get-tuple-element.2082), channel_id=1, replica_groups=mesh['dp'=8,'tensor'=4] {'dp'}, dimensions={1}, use_global_device_ids=true | all-gather | bytes 147456 | tf_op jit(solution)/shard_map/while/body/eval_jaxpr/all_gather | solution.py:39
  701.6 31.2 %all_gather.147 = bf16[3,512,128]{2,1,0:T(8,128)(2,1)S(1)} all-gather(bf16[3,64,128]{2,1,0:T(8,128)(2,1)} %get-tuple-element.2077), channel_id=1, replica_groups=mesh['dp'=8,'tensor'=4] {'dp'}, dimensions={1}, use_global_device_ids=true | all-gather | bytes 442368 | tf_op jit(solution)/shard_map/while/body/eval_jaxpr/all_gather | solution.py:38
  735.7 12.2 while.160
  751.7 27.0 %reduce-scatter.29.cloned.1.call-done = f32[256,512]{1,0:T(8,128)} async-done(((f32[1024,512]{1,0:T(8,128)}), f32[256,512]{1,0:T(8,128)}) %reduce-scatter.29.cloned.1.call-update) | async-done | bytes 524304 | tf_op jit(solution)/shard_map/while/body/eval_jaxpr/reduce_scatter | solution.py:95
  781.7 30.6 %all_gather.154 = bf16[128,512]{0,1:T(8,128)(2,1)S(1)} all-gather(bf16[128,64]{0,1:T(8,128)(2,1)S(1)} %copy-done.65), channel_id=1, replica_groups=mesh['dp'=8,'tensor'=4] {'dp'}, dimensions={1}, use_global_device_ids=true | all-gather | bytes 147456 | tf_op jit(solution)/shard_map/while/body/eval_jaxpr/all_gather | solution.py:42
  812.3 30.5 %all_gather.150 = bf16[512,128]{1,0:T(8,128)(2,1)S(1)} all-gather(bf16[64,128]{1,0:T(8,128)(2,1)S(1)} %copy-done.64), channel_id=1, replica_groups=mesh['dp'=8,'tensor'=4] {'dp'}, dimensions={0}, use_global_device_ids=true | all-gather | bytes 147456 | tf_op jit(solution)/shard_map/while/body/eval_jaxpr/all_gather | solution.py:40
  842.8 30.7 %all_gather.151 = bf16[2,512,128]{2,1,0:T(8,128)(2,1)S(1)} all-gather(bf16[2,64,128]{2,1,0:T(8,128)(2,1)S(1)} %copy-done.50), channel_id=1, replica_groups=mesh['dp'=8,'tensor'=4] {'dp'}, dimensions={1}, use_global_device_ids=true | all-gather | bytes 294912 | tf_op jit(solution)/shard_map/while/body/eval_jaxpr/all_gather | solution.py:41
  877.8 8.1 while.161
  891.8 28.5 %reduce-scatter.31.cloned.1.call-done = f32[256,512]{1,0:T(8,128)} async-done(((f32[1024,512]{1,0:T(8,128)}), f32[256,512]{1,0:T(8,128)}) %reduce-scatter.31.cloned.1.call-update) | async-done | bytes 524304 | tf_op jit(solution)/shard_map/while/body/eval_jaxpr/reduce_scatter | solution.py:95
  922.7 33.6 %all_gather.156 = bf16[512,512]{1,0:T(8,128)(2,1)} all-gather(bf16[64,512]{1,0:T(8,128)(2,1)S(1)} %copy-done.38), channel_id=1, replica_groups=mesh['dp'=8,'tensor'=4] {'dp'}, dimensions={0}, use_global_device_ids=true | all-gather | bytes 589824 | tf_op jit(solution)/shard_map/while/body/eval_jaxpr/all_gather | solution.py:43
  956.3 31.2 %all_gather.153 = bf16[512,512]{0,1:T(8,128)(2,1)S(1)} all-gather(bf16[512,64]{0,1:T(8,128)(2,1)S(1)} %copy-done.37), channel_id=1, replica_groups=mesh['dp'=8,'tensor'=4] {'dp'}, dimensions={1}, use_global_device_ids=true | all-gather | bytes 589824 | tf_op jit(solution)/shard_map/while/body/eval_jaxpr/all_gather | solution.py:44
  987.5 3.5 fusion.336
  991.0 5.3 fusion.340
  999.4 31.6 %reduce-scatter.33.cloned.1.call-done = f32[256,512]{1,0:T(8,128)} async-done(((f32[1024,512]{1,0:T(8,128)}), f32[256,512]{1,0:T(8,128)}) %reduce-scatter.33.cloned.1.call-update) | async-done | bytes 524304 | tf_op jit(solution)/shard_map/while/body/eval_jaxpr/reduce_scatter | solution.py:104
  1036.0 16.8 all-gather.22.cloned.1.call-done
  1059.2 13.5 while.162
  1074.0 2.8 fusion.344
  1076.9 31.5 %reduce-scatter.35.cloned.1.call-done = f32[256,512]{1,0:T(8,128)} async-done(((f32[1024,512]{1,0:T(8,128)}), f32[256,512]{1,0:T(8,128)}) %reduce-scatter.35.cloned.1.call-update) | async-done | bytes 524304 | tf_op jit(solution)/shard_map/while/body/eval_jaxpr/reduce_scatter | solution.py:342
  1113.8 3.9 fusion.351
  1121.6 9.0 all-gather.24.cloned.1.call-done
  1133.7 21.7 %while.163 = (s32[]{:T(128)}, f32[1024,2,64]{0,2,1:T(8,128)S(1)}, f32[1024,2,64]{0,2,1:T(8,128)}, bf16[2,512,2,64]{1,3,2,0:T(8,128)(2,1)}, bf16[2,512,2,64]{1,3,...) while((s32[]{:T(128)}, f32[1024,2,64]{0,2,1:T(8,128)S(1)}, ...), condition=%wide.region_28.28_spmd.clone, body=%wide.region_26.27_spmd.clone.sunk | while | flops 688587264 | bytes 37259468 | solution.py:191
  1147.1 3.2 fusion.389
  1161.1 3.5 convolution_add_fusion.13
  1175.7 22.8 %reduce-scatter.41.cloned.1.call-done = f32[256,512]{1,0:T(8,128)} async-done(((f32[1024,512]{1,0:T(8,128)}), f32[256,512]{1,0:T(8,128)}) %reduce-scatter.41.cloned.1.call-update) | async-done | bytes 524304 | tf_op jit(solution)/shard_map/while/body/eval_jaxpr/reduce_scatter | solution.py:343
  1202.8 3.1 fusion.347
  1205.9 26.6 %reduce-scatter.37.cloned.1.call-done = f32[256,512]{1,0:T(8,128)} async-done(((f32[1024,512]{1,0:T(8,128)}), f32[256,512]{1,0:T(8,128)}) %reduce-scatter.37.cloned.1.call-update) | async-done | bytes 524304 | tf_op jit(solution)/shard_map/while/body/eval_jaxpr/reduce_scatter | solution.py:104
  1251.9 37.1 %all-reduce.19 = (f32[512]{0:T(512)S(1)}, f32[512]{0:T(512)S(1)}, f32[512]{0:T(512)S(1)}, f32[512]{0:T(512)S(1)}, f32[512]{0:T(512)S(1)}, /*index=5*/f32[512]{0:T(512)S(1)}) all-reduce(f32[512]{0:T(512)S(1)} %copy-done.95, f32[512]{0:T(512)S(1)} %copy-done.92, ...), channel_id=17, replica_groups=mesh['dp'=8,'tensor'=4] {'dp'}, use_global_device_ids=true, to_apply=%region_48.49.clone | all-reduce | flops 3072 | bytes 24576
  1289.4 6.4 all-reduce.20
  1295.9 9.5 reduce-scatter.19.cloned.1.call-done
  1305.4 64.1 %reduce-scatter.17.cloned.1.call-done = f32[128,64]{0,1:T(8,128)} async-done(((f32[128,512]{0,1:T(8,128)}), f32[128,64]{0,1:T(8,128)}) %reduce-scatter.17.cloned.1.call-update) | async-done | bytes 32784 | tf_op jit(solution)/shard_map/reduce_scatter | solution.py:71
  1369.5 64.2 %reduce-scatter.23.cloned.1.call-done = f32[128,64]{0,1:T(8,128)} async-done(((f32[128,512]{0,1:T(8,128)}), f32[128,64]{0,1:T(8,128)}) %reduce-scatter.23.cloned.1.call-update) | async-done | bytes 32784 | tf_op jit(solution)/shard_map/reduce_scatter | solution.py:74
  1433.7 65.0 %reduce-scatter.21.cloned.1.call-done = f32[2,64,128]{2,1,0:T(8,128)} async-done(((f32[2,512,128]{2,1,0:T(8,128)}), f32[2,64,128]{2,1,0:T(8,128)}) %reduce-scatter.21.cloned.1.call-update) | async-done | bytes 65552 | tf_op jit(solution)/shard_map/reduce_scatter | solution.py:73
  1498.7 66.6 %reduce-scatter.15.cloned.1.call-done = f32[3,64,128]{2,1,0:T(8,128)} async-done(((f32[3,512,128]{2,1,0:T(8,128)}), f32[3,64,128]{2,1,0:T(8,128)}) %reduce-scatter.15.cloned.1.call-update) | async-done | bytes 98320 | tf_op jit(solution)/shard_map/reduce_scatter | solution.py:70
  1565.3 66.6 %reduce-scatter.25.cloned.1.call-done = f32[64,512]{1,0:T(8,128)} async-done(((f32[512,512]{1,0:T(8,128)}), f32[64,512]{1,0:T(8,128)}) %reduce-scatter.25.cloned.1.call-update) | async-done | bytes 131088 | tf_op jit(solution)/shard_map/reduce_scatter | solution.py:75
  1631.9 66.8 %reduce-scatter.27.cloned.1.call-done = f32[512,64]{0,1:T(8,128)} async-done(((f32[512,512]{0,1:T(8,128)}), f32[512,64]{0,1:T(8,128)}) %reduce-scatter.27.cloned.1.call-update) | async-done | bytes 131088 | tf_op jit(solution)/shard_map/reduce_scatter | solution.py:76
  (856 shorter events, 283.5 us)
Async XLA Ops:
  32.2 98.4 %all-gather.12.cloned.1.call-start = ((), (), s32[]{:S(2)}) async-start(), calls=%async_computation.21 | async-start | bytes 1310720 | tf_op jit(solution)/shard_map/while/body/eval_jaxpr/all_gather | solution.py:87
  33.3 66.0 %copy-start.44 = (f32[256]{0:T(256)}, f32[256]{0:T(256)S(1)}, u32[]{:S(2)}) copy-start(f32[256]{0:T(256)S(1)} %broadcast_multiply_fusion.6) | copy-start | bytes 3076 | tf_op jit(solution)/shard_map/while
  34.5 64.8 %copy-start.58 = (f32[256]{0:T(256)}, f32[256]{0:T(256)S(1)}, u32[]{:S(2)}) copy-start(f32[256]{0:T(256)S(1)} %fusion.326) | copy-start | bytes 3076 | tf_op jit(solution)/shard_map/while
  67.3 110.1 %reduce-scatter.29.cloned.1.call-start = ((), (), s32[]{:S(2)}) async-start(), calls=%async_computation.22 | async-start | bytes 2621440 | tf_op jit(solution)/shard_map/while/body/eval_jaxpr/reduce_scatter | solution.py:95
  146.8 64.2 %copy-start.64 = (bf16[64,128]{1,0:T(8,128)(2,1)S(1)}, bf16[64,128]{1,0:T(8,128)(2,1)}, u32[]{:S(2)}) copy-start(bf16[64,128]{1,0:T(8,128)(2,1)} %get-tuple-element.2085) | copy-start | bytes 49156 | tf_op jit(solution)/shard_map/while
  146.8 94.7 %copy-start.50 = (bf16[2,64,128]{2,1,0:T(8,128)(2,1)S(1)}, bf16[2,64,128]{2,1,0:T(8,128)(2,1)}, u32[]{:S(2)}) copy-start(bf16[2,64,128]{2,1,0:T(8,128)(2,1)} %get-tuple-element.2087) | copy-start | bytes 98308 | tf_op jit(solution)/shard_map/while
  148.6 123.6 %all-gather.16.cloned.1.call-start = ((), (), s32[]{:S(2)}) async-start(), calls=%async_computation.24 | async-start | bytes 1310720 | tf_op jit(solution)/shard_map/while/body/eval_jaxpr/all_gather | solution.py:279
  149.4 124.7 %all-gather.14.cloned.1.call-start = ((), (), s32[]{:S(2)}) async-start(), calls=%async_computation.23 | async-start | bytes 1310720 | tf_op jit(solution)/shard_map/while/body/eval_jaxpr/all_gather | solution.py:278
  149.5 126.5 %copy-start.46 = (f32[512]{0:T(512)}, f32[512]{0:T(512)S(1)}, u32[]{:S(2)}) copy-start(f32[512]{0:T(512)S(1)} %convert_element_type.395) | copy-start | bytes 6148 | tf_op jit(solution)/shard_map/while
  178.6 97.8 %copy-start.54 = (f32[256]{0:T(256)}, f32[256]{0:T(256)S(1)}, u32[]{:S(2)}) copy-start(f32[256]{0:T(256)S(1)} %broadcast_multiply_fusion.7) | copy-start | bytes 3076 | tf_op jit(solution)/shard_map/while
  178.8 97.6 %copy-start.70 = (f32[256]{0:T(256)}, f32[256]{0:T(256)S(1)}, u32[]{:S(2)}) copy-start(f32[256]{0:T(256)S(1)} %multiply_reduce_fusion.14) | copy-start | bytes 3076 | tf_op jit(solution)/shard_map/while
  178.8 97.6 %copy-start.60 = (f32[256]{0:T(256)}, f32[256]{0:T(256)S(1)}, u32[]{:S(2)}) copy-start(f32[256]{0:T(256)S(1)} %fusion.332) | copy-start | bytes 3076 | tf_op jit(solution)/shard_map/while
  179.7 139.2 %reduce-scatter.31.cloned.1.call-start = ((), (), s32[]{:S(2)}) async-start(), calls=%async_computation.26 | async-start | bytes 2621440 | tf_op jit(solution)/shard_map/while/body/eval_jaxpr/reduce_scatter | solution.py:95
  285.6 69.4 %copy-start.37 = (bf16[512,64]{0,1:T(8,128)(2,1)S(1)}, bf16[512,64]{0,1:T(8,128)(2,1)}, u32[]{:S(2)}) copy-start(bf16[512,64]{0,1:T(8,128)(2,1)} %get-tuple-element.2081) | copy-start | bytes 196612 | tf_op jit(solution)/shard_map/while
  287.4 98.8 %all-gather.18.cloned.1.call-start = ((), (), s32[]{:S(2)}) async-start(), calls=%async_computation.25 | async-start | bytes 1310720 | tf_op jit(solution)/shard_map/while/body/eval_jaxpr/all_gather | solution.py:91
  289.0 100.7 %all-gather.20.cloned.1.call-start = ((), (), s32[]{:S(2)}) async-start(), calls=%async_computation.27 | async-start | bytes 1310720 | tf_op jit(solution)/shard_map/while/body/eval_jaxpr/all_gather | solution.py:87
  289.7 65.2 %copy-start.48 = (f32[512]{0:T(512)}, f32[512]{0:T(512)S(1)}, u32[]{:S(2)}) copy-start(f32[512]{0:T(512)S(1)} %convert_element_type.397) | copy-start | bytes 6148 | tf_op jit(solution)/shard_map/while
  321.3 108.5 %reduce-scatter.33.cloned.1.call-start = ((), (), s32[]{:S(2)}) async-start(), calls=%async_computation.28 | async-start | bytes 2621440 | tf_op jit(solution)/shard_map/while/body/eval_jaxpr/reduce_scatter | solution.py:104
  398.0 53.5 %all-gather.22.cloned.1.call-start = ((), (), s32[]{:S(2)}) async-start(), calls=%async_computation.29 | async-start | bytes 1310720 | tf_op jit(solution)/shard_map/while/body/eval_jaxpr/all_gather | solution.py:91
  434.6 72.5 %reduce-scatter.35.cloned.1.call-start = ((), (), s32[]{:S(2)}) async-start(), calls=%async_computation.30 | async-start | bytes 2621440 | tf_op jit(solution)/shard_map/while/body/eval_jaxpr/reduce_scatter | solution.py:342
  475.6 53.8 %all-gather.24.cloned.1.call-start = ((), (), s32[]{:S(2)}) async-start(), calls=%async_computation.31 | async-start | bytes 1310720 | tf_op jit(solution)/shard_map/while/body/eval_jaxpr/all_gather | solution.py:91
  512.4 52.8 %reduce-scatter.39.cloned.1.call-start = ((), (), s32[]{:S(2)}) async-start(), calls=%async_computation.33 | async-start | bytes 2621440 | tf_op jit(solution)/shard_map/while/body/eval_jaxpr/reduce_scatter | solution.py:95
  516.4 80.9 %reduce-scatter.41.cloned.1.call-start = ((), (), s32[]{:S(2)}) async-start(), calls=%async_computation.34 | async-start | bytes 2621440 | tf_op jit(solution)/shard_map/while/body/eval_jaxpr/reduce_scatter | solution.py:343
  520.3 110.9 %reduce-scatter.37.cloned.1.call-start = ((), (), s32[]{:S(2)}) async-start(), calls=%async_computation.32 | async-start | bytes 2621440 | tf_op jit(solution)/shard_map/while/body/eval_jaxpr/reduce_scatter | solution.py:104
  573.0 58.2 %copy-start.1 = (bf16[2,256,512]{2,1,0:T(8,128)(2,1)S(1)}, bf16[2,256,512]{2,1,0:T(8,128)(2,1)}, u32[]{:S(2)}) copy-start(bf16[2,256,512]{2,1,0:T(8,128)(2,1)} %get-tuple-element.2074) | copy-start | bytes 1572868 | tf_op jit(solution)/shard_map/while
  573.0 58.2 %copy-start.40 = (f32[512]{0:T(512)S(1)}, f32[512]{0:T(512)}, u32[]{:S(2)}) copy-start(f32[512]{0:T(512)} %copy-done.39) | copy-start | bytes 6148 | tf_op jit(solution)/shard_map/while
  573.0 58.2 %copy-start.45 = (f32[256]{0:T(256)S(1)}, f32[256]{0:T(256)}, u32[]{:S(2)}) copy-start(f32[256]{0:T(256)} %copy-done.44) | copy-start | bytes 3076 | tf_op jit(solution)/shard_map/while
  573.0 59.5 %copy-start.69 = (f32[256]{0:T(256)S(1)}, f32[256]{0:T(256)}, u32[]{:S(2)}) copy-start(f32[256]{0:T(256)} %copy-done.68) | copy-start | bytes 3076 | tf_op jit(solution)/shard_map/while
  573.0 59.5 %copy-start.59 = (f32[256]{0:T(256)S(1)}, f32[256]{0:T(256)}, u32[]{:S(2)}) copy-start(f32[256]{0:T(256)} %copy-done.58) | copy-start | bytes 3076 | tf_op jit(solution)/shard_map/while
  573.1 60.8 %copy-start.85 = (f32[512]{0:T(512)}, f32[512]{0:T(512)S(1)}, u32[]{:S(2)}) copy-start(f32[512]{0:T(512)S(1)} %get-tuple-element.2068) | copy-start | bytes 6148 | tf_op jit(solution)/shard_map/while
  573.1 60.8 %copy-start.88 = (f32[512]{0:T(512)}, f32[512]{0:T(512)S(1)}, u32[]{:S(2)}) copy-start(f32[512]{0:T(512)S(1)} %get-tuple-element.2067) | copy-start | bytes 6148 | tf_op jit(solution)/shard_map/while
  636.2 96.5 %all-gather.12.cloned.1.call-start = ((), (), s32[]{:S(2)}) async-start(), calls=%async_computation.21 | async-start | bytes 1310720 | tf_op jit(solution)/shard_map/while/body/eval_jaxpr/all_gather | solution.py:87
  637.3 64.3 %copy-start.44 = (f32[256]{0:T(256)}, f32[256]{0:T(256)S(1)}, u32[]{:S(2)}) copy-start(f32[256]{0:T(256)S(1)} %broadcast_multiply_fusion.6) | copy-start | bytes 3076 | tf_op jit(solution)/shard_map/while
  638.5 63.1 %copy-start.58 = (f32[256]{0:T(256)}, f32[256]{0:T(256)S(1)}, u32[]{:S(2)}) copy-start(f32[256]{0:T(256)S(1)} %fusion.326) | copy-start | bytes 3076 | tf_op jit(solution)/shard_map/while
  669.6 109.1 %reduce-scatter.29.cloned.1.call-start = ((), (), s32[]{:S(2)}) async-start(), calls=%async_computation.22 | async-start | bytes 2621440 | tf_op jit(solution)/shard_map/while/body/eval_jaxpr/reduce_scatter | solution.py:95
  749.0 63.3 %copy-start.64 = (bf16[64,128]{1,0:T(8,128)(2,1)S(1)}, bf16[64,128]{1,0:T(8,128)(2,1)}, u32[]{:S(2)}) copy-start(bf16[64,128]{1,0:T(8,128)(2,1)} %get-tuple-element.2085) | copy-start | bytes 49156 | tf_op jit(solution)/shard_map/while
  749.0 93.8 %copy-start.50 = (bf16[2,64,128]{2,1,0:T(8,128)(2,1)S(1)}, bf16[2,64,128]{2,1,0:T(8,128)(2,1)}, u32[]{:S(2)}) copy-start(bf16[2,64,128]{2,1,0:T(8,128)(2,1)} %get-tuple-element.2087) | copy-start | bytes 98308 | tf_op jit(solution)/shard_map/while
  750.8 122.7 %all-gather.16.cloned.1.call-start = ((), (), s32[]{:S(2)}) async-start(), calls=%async_computation.24 | async-start | bytes 1310720 | tf_op jit(solution)/shard_map/while/body/eval_jaxpr/all_gather | solution.py:279
  751.7 123.8 %all-gather.14.cloned.1.call-start = ((), (), s32[]{:S(2)}) async-start(), calls=%async_computation.23 | async-start | bytes 1310720 | tf_op jit(solution)/shard_map/while/body/eval_jaxpr/all_gather | solution.py:278
  751.7 125.6 %copy-start.46 = (f32[512]{0:T(512)}, f32[512]{0:T(512)S(1)}, u32[]{:S(2)}) copy-start(f32[512]{0:T(512)S(1)} %convert_element_type.395) | copy-start | bytes 6148 | tf_op jit(solution)/shard_map/while
  779.9 97.8 %copy-start.54 = (f32[256]{0:T(256)}, f32[256]{0:T(256)S(1)}, u32[]{:S(2)}) copy-start(f32[256]{0:T(256)S(1)} %broadcast_multiply_fusion.7) | copy-start | bytes 3076 | tf_op jit(solution)/shard_map/while
  780.1 97.7 %copy-start.70 = (f32[256]{0:T(256)}, f32[256]{0:T(256)S(1)}, u32[]{:S(2)}) copy-start(f32[256]{0:T(256)S(1)} %multiply_reduce_fusion.14) | copy-start | bytes 3076 | tf_op jit(solution)/shard_map/while
  780.1 97.6 %copy-start.60 = (f32[256]{0:T(256)}, f32[256]{0:T(256)S(1)}, u32[]{:S(2)}) copy-start(f32[256]{0:T(256)S(1)} %fusion.332) | copy-start | bytes 3076 | tf_op jit(solution)/shard_map/while
  781.0 139.2 %reduce-scatter.31.cloned.1.call-start = ((), (), s32[]{:S(2)}) async-start(), calls=%async_computation.26 | async-start | bytes 2621440 | tf_op jit(solution)/shard_map/while/body/eval_jaxpr/reduce_scatter | solution.py:95
  886.9 69.4 %copy-start.37 = (bf16[512,64]{0,1:T(8,128)(2,1)S(1)}, bf16[512,64]{0,1:T(8,128)(2,1)}, u32[]{:S(2)}) copy-start(bf16[512,64]{0,1:T(8,128)(2,1)} %get-tuple-element.2081) | copy-start | bytes 196612 | tf_op jit(solution)/shard_map/while
  888.8 98.8 %all-gather.18.cloned.1.call-start = ((), (), s32[]{:S(2)}) async-start(), calls=%async_computation.25 | async-start | bytes 1310720 | tf_op jit(solution)/shard_map/while/body/eval_jaxpr/all_gather | solution.py:91
  890.3 100.7 %all-gather.20.cloned.1.call-start = ((), (), s32[]{:S(2)}) async-start(), calls=%async_computation.27 | async-start | bytes 1310720 | tf_op jit(solution)/shard_map/while/body/eval_jaxpr/all_gather | solution.py:87
  891.1 65.2 %copy-start.48 = (f32[512]{0:T(512)}, f32[512]{0:T(512)S(1)}, u32[]{:S(2)}) copy-start(f32[512]{0:T(512)S(1)} %convert_element_type.397) | copy-start | bytes 6148 | tf_op jit(solution)/shard_map/while
  922.6 108.5 %reduce-scatter.33.cloned.1.call-start = ((), (), s32[]{:S(2)}) async-start(), calls=%async_computation.28 | async-start | bytes 2621440 | tf_op jit(solution)/shard_map/while/body/eval_jaxpr/reduce_scatter | solution.py:104
  999.4 53.4 %all-gather.22.cloned.1.call-start = ((), (), s32[]{:S(2)}) async-start(), calls=%async_computation.29 | async-start | bytes 1310720 | tf_op jit(solution)/shard_map/while/body/eval_jaxpr/all_gather | solution.py:91
  1035.9 72.5 %reduce-scatter.35.cloned.1.call-start = ((), (), s32[]{:S(2)}) async-start(), calls=%async_computation.30 | async-start | bytes 2621440 | tf_op jit(solution)/shard_map/while/body/eval_jaxpr/reduce_scatter | solution.py:342
  1076.8 53.8 %all-gather.24.cloned.1.call-start = ((), (), s32[]{:S(2)}) async-start(), calls=%async_computation.31 | async-start | bytes 1310720 | tf_op jit(solution)/shard_map/while/body/eval_jaxpr/all_gather | solution.py:91
  1113.7 53.1 %reduce-scatter.39.cloned.1.call-start = ((), (), s32[]{:S(2)}) async-start(), calls=%async_computation.33 | async-start | bytes 2621440 | tf_op jit(solution)/shard_map/while/body/eval_jaxpr/reduce_scatter | solution.py:95
  1117.7 80.8 %reduce-scatter.41.cloned.1.call-start = ((), (), s32[]{:S(2)}) async-start(), calls=%async_computation.34 | async-start | bytes 2621440 | tf_op jit(solution)/shard_map/while/body/eval_jaxpr/reduce_scatter | solution.py:343
  1121.6 110.9 %reduce-scatter.37.cloned.1.call-start = ((), (), s32[]{:S(2)}) async-start(), calls=%async_computation.32 | async-start | bytes 2621440 | tf_op jit(solution)/shard_map/while/body/eval_jaxpr/reduce_scatter | solution.py:104
  1175.7 59.5 %copy-start.85 = (f32[512]{0:T(512)}, f32[512]{0:T(512)S(1)}, u32[]{:S(2)}) copy-start(f32[512]{0:T(512)S(1)} %get-tuple-element.2068) | copy-start | bytes 6148 | tf_op jit(solution)/shard_map/while
  1175.7 59.5 %copy-start.88 = (f32[512]{0:T(512)}, f32[512]{0:T(512)S(1)}, u32[]{:S(2)}) copy-start(f32[512]{0:T(512)S(1)} %get-tuple-element.2067) | copy-start | bytes 6148 | tf_op jit(solution)/shard_map/while
  1239.6 65.8 %reduce-scatter.19.cloned.1.call-start = ((), (), s32[]{:S(2)}) async-start(), calls=%async_computation.16 | async-start | bytes 294912 | tf_op jit(solution)/shard_map/reduce_scatter | solution.py:72
  1240.2 129.3 %reduce-scatter.17.cloned.1.call-start = ((), (), s32[]{:S(2)}) async-start(), calls=%async_computation.15 | async-start | bytes 294912 | tf_op jit(solution)/shard_map/reduce_scatter | solution.py:71
  1242.0 191.6 %reduce-scatter.23.cloned.1.call-start = ((), (), s32[]{:S(2)}) async-start(), calls=%async_computation.18 | async-start | bytes 294912 | tf_op jit(solution)/shard_map/reduce_scatter | solution.py:74
  1244.0 254.7 %reduce-scatter.21.cloned.1.call-start = ((), (), s32[]{:S(2)}) async-start(), calls=%async_computation.17 | async-start | bytes 589824 | tf_op jit(solution)/shard_map/reduce_scatter | solution.py:73
  1246.1 319.3 %reduce-scatter.15.cloned.1.call-start = ((), (), s32[]{:S(2)}) async-start(), calls=%async_computation.14 | async-start | bytes 884736 | tf_op jit(solution)/shard_map/reduce_scatter | solution.py:70
  1248.4 383.4 %reduce-scatter.25.cloned.1.call-start = ((), (), s32[]{:S(2)}) async-start(), calls=%async_computation.19 | async-start | bytes 1179648 | tf_op jit(solution)/shard_map/reduce_scatter | solution.py:75
  1249.2 449.5 %reduce-scatter.27.cloned.1.call-start = ((), (), s32[]{:S(2)}) async-start(), calls=%async_computation.20 | async-start | bytes 1179648 | tf_op jit(solution)/shard_map/reduce_scatter | solution.py:76
  (173 other events, 2961.0 us)
Sparse Core Ops, SparseCore 0:
  67.4 13.9 all-gather.11
  148.7 28.6 reduce-scatter.28
  179.0 16.7 all-gather.15
  197.3 16.7 all-gather.13
  287.5 31.3 reduce-scatter.30
  320.4 16.7 all-gather.17
  338.7 16.7 all-gather.19
  398.2 31.5 reduce-scatter.32
  434.8 16.7 all-gather.21
  475.7 31.3 reduce-scatter.34
  512.6 16.7 all-gather.23
  531.7 31.4 reduce-scatter.38
  565.9 31.4 reduce-scatter.40
  599.7 31.4 reduce-scatter.36
  669.7 13.0 all-gather.11
  751.0 27.7 reduce-scatter.28
  780.2 16.7 all-gather.15
  798.5 16.7 all-gather.13
  888.9 31.3 reduce-scatter.30
  921.7 16.7 all-gather.17
  940.0 16.7 all-gather.19
  999.5 31.5 reduce-scatter.32
  1036.1 16.7 all-gather.21
  1077.0 31.4 reduce-scatter.34
  1113.9 16.7 all-gather.23
  1133.0 31.4 reduce-scatter.38
  1167.0 31.4 reduce-scatter.40
  1201.0 31.4 reduce-scatter.36
Sparse Core Ops, SparseCore 1:
  1244.0 61.3 reduce-scatter.18
  1309.1 60.3 reduce-scatter.16
  1373.3 60.3 reduce-scatter.22
  1437.6 61.0 reduce-scatter.20
  1503.0 62.3 reduce-scatter.14
  1569.3 62.5 reduce-scatter.24
  1636.1 62.5 reduce-scatter.26
where the time goes:
time: 1710 us
  waiting for transfers between devices  795 us (46%)
  blocking collectives  527 us (31%)
  matrix products  166 us (10%)
  other arithmetic  91.1 us (5%)
  local copies, waits for them, and re-layouts  73.3 us (4%)
  loops' own time  36.5 us (2%)
    reduce_scatter x4, waiting for transfers between devices, input_grad(): lax.psum_scatter(grad_term(jnp.int32(0), own_rows * lax.axis_size('tensor...  117 us
    reduce_scatter x6, waiting for transfers between devices, branch_sum(): lax.psum_scatter(jnp.dot(mixture, weight, preferred_element_type=jnp.floa...  112 us
    all_gather x2, blocking collectives, gather_weights(): lax.all_gather(ffn_up, 'dp', axis=0, tiled=True)  67.2 us
    reduce_scatter x1, waiting for transfers between devices, reduce_grads(): lax.psum_scatter(grad_down, 'dp', scatter_dimension=1, tiled=True)  66.8 us
    reduce_scatter x1, waiting for transfers between devices, reduce_grads(): lax.psum_scatter(grad_qkv, 'dp', scatter_dimension=1, tiled=True)  66.6 us
    reduce_scatter x1, waiting for transfers between devices, reduce_grads(): lax.psum_scatter(grad_up, 'dp', scatter_dimension=0, tiled=True)  66.6 us
    reduce_scatter x1, waiting for transfers between devices, reduce_grads(): lax.psum_scatter(grad_pair, 'dp', scatter_dimension=1, tiled=True)  65 us
    reduce_scatter x1, waiting for transfers between devices, reduce_grads(): lax.psum_scatter(grad_cross, 'dp', scatter_dimension=1, tiled=True)  64.2 us
  transfers between devices with their start and end apart: 35, of which 23 were waited for; matrix products, arithmetic and copies ran while one was open for 9% of the time, Pallas kernels for 0%

commit v1 on v0

--- a/solution.py
+++ b/solution.py
@@ -7,6 +7,27 @@
 EPSILON = 1e-05
 MASKED = -1e30
 BLOCK_ROWS = 512
+
+
+def gather_around(x, axis, dim):
+    size, index, width = (lax.axis_size(axis), lax.axis_index(axis), x.shape[dim])
+    right = [(i, (i + 1) % size) for i in range(size)]
+    left = [(i, (i - 1) % size) for i in range(size)]
+    out = jnp.zeros((*x.shape[:dim], size * width, *x.shape[dim + 1 :]), x.dtype)
+    out = lax.dynamic_update_slice_in_dim(out, x, index * width, axis=dim)
+    from_left = from_right = x
+    half = size // 2
+    for step in range(1, half + 1):
+        from_left = lax.ppermute(from_left, axis, right)
+        out = lax.dynamic_update_slice_in_dim(
+            out, from_left, (index - step) % size * width, axis=dim
+        )
+        if step < size - half:
+            from_right = lax.ppermute(from_right, axis, left)
+            out = lax.dynamic_update_slice_in_dim(
+                out, from_right, (index + step) % size * width, axis=dim
+            )
+    return out
 
 
 def layer_norm(values, gain_vec, bias_vec):
@@ -88,7 +109,7 @@
 
 
 def grad_rows(own_part):
-    return lax.all_gather(own_part, "tensor", axis=0, tiled=True)
+    return gather_around(own_part, "tensor", 0)
 
 
 def branch_sum(mixture, weight):

time: 1710 us -> 1660 us (0.971)
  waiting for transfers between devices: 795 us -> 726 us
  local copies, waits for them, and re-layouts: 73.3 us -> 98.4 us
  loops' own time: 36.5 us -> 13.2 us
    all_gather x6 -> x0, waiting for transfers between devices: 51.6 us -> none  [grad_rows(): return lax.all_gather(own_part, 'tensor', axis=0, tiled=True)]
    reduce_scatter x2, waiting for transfers between devices: 47 us -> 5 us  [advance(): lax.psum_scatter(back_memory, 'tensor', scatter_dimension=0, tiled=True)]
    ppermute x0 -> x18, waiting for transfers between devices: none -> 30.1 us  [the longest x12 30.1 us: gather_around(): from_left = lax.ppermute(from_left, axis, right)]
    dynamic_update_slice x0 -> x18, local copies, waits for them, and re-layouts: none -> 24.4 us  [the longest x12 16.3 us: gather_around(): lax.dynamic_update_slice_in_dim(out, from_left, (index - step) % size * w...]
    another operation x1, loops' own time: 30.4 us -> 7.02 us  [body(): lax.scan(advance, accum_init, (inputs, memory, tgt_len, src_len, cotangent))]
  transfers between devices with their start and end apart: 35 -> 47, of which waited for: 23 -> 27; matrix products, arithmetic and copies ran while one was open for 9% -> 11% of each run, Pallas kernels for 0% -> 0%
where the time goes in v1:
time: 1660 us; the launch traced here: 1650 us
  waiting for transfers between devices  726 us (44%)
  blocking collectives  527 us (32%)
  matrix products  166 us (10%)
  local copies, waits for them, and re-layouts  98.4 us (6%)
  other arithmetic  92.5 us (6%)
  between operations  16.7 us (1%)
    reduce_scatter x4, waiting for transfers between devices, input_grad(): lax.psum_scatter(grad_term(jnp.int32(0), own_rows * lax.axis_size('tensor...  117 us
    reduce_scatter x6, waiting for transfers between devices, branch_sum(): lax.psum_scatter(jnp.dot(mixture, weight, preferred_element_type=jnp.floa...  115 us
    reduce_scatter x1, waiting for transfers between devices, reduce_grads(): lax.psum_scatter(grad_down, 'dp', scatter_dimension=1, tiled=True)  66.8 us
    reduce_scatter x1, waiting for transfers between devices, reduce_grads(): lax.psum_scatter(grad_qkv, 'dp', scatter_dimension=1, tiled=True)  66.5 us
    reduce_scatter x1, waiting for transfers between devices, reduce_grads(): lax.psum_scatter(grad_up, 'dp', scatter_dimension=0, tiled=True)  66.5 us
    all_gather x2, blocking collectives, gather_weights(): lax.all_gather(ffn_down, 'dp', axis=1, tiled=True)  66.4 us
    reduce_scatter x1, waiting for transfers between devices, reduce_grads(): lax.psum_scatter(grad_pair, 'dp', scatter_dimension=1, tiled=True)  65.1 us
    reduce_scatter x1, waiting for transfers between devices, reduce_grads(): lax.psum_scatter(grad_cross, 'dp', scatter_dimension=1, tiled=True)  64.2 us
  transfers between devices with their start and end apart: 47, of which 27 were waited for; matrix products, arithmetic and copies ran while one was open for 11% of the time, Pallas kernels for 0%

profile of v1, /device:TPU:0, one launch (start us, length us, event | category | flops | bytes accessed | tf_op | source)
XLA Modules:
  0.0 1653.6 jit_solution(10142993376522345186)
XLA Ops:
  8.2 1178.7 %while.159 = (s32[]{:T(128)}, f32[3,512,128]{1,2,0:T(8,128)}, f32[128,512]{1,0:T(8,128)}, f32[512,128]{1,0:T(8,128)}, f32[2,512,128]{1,2,0:T(8,128)}, /*index=5*...) while((s32[]{:T(128)}, f32[3,512,128]{1,2,0:T(8,128)}, ...), condition=%wide.region_40.41_spmd.clone, body=%wide.region_0.40_spmd.clone.sunk | while | flops 8421522944 | bytes 374971648 | solution.py:408
  18.0 23.9 %all-reduce.22 = (bf16[512]{0:T(512)(128)(2,1)S(1)}, bf16[512]{0:T(512)(128)(2,1)S(1)}, bf16[512]{0:T(512)(128)(2,1)S(1)}, bf16[512]{0:T(512)(128)(2,1)S(1)}, bf...) all-reduce(bf16[512]{0:T(512)(128)(2,1)S(1)} %dynamic-update-slice.18, ...), channel_id=1, replica_groups=mesh['dp'=8,'tensor'=4] {'dp'}, use_global_device_ids=true, to_apply=%add.1 | all-reduce | flops 3072 | bytes 12288 | tf_op jit(solution)/shard_map/while
  45.1 30.7 %all_gather.124 = bf16[128,512]{0,1:T(8,128)(2,1)S(1)} all-gather(bf16[128,64]{0,1:T(8,128)(2,1)} %get-tuple-element.2109), channel_id=1, replica_groups=mesh['dp'=8,'tensor'=4] {'dp'}, dimensions={1}, use_global_device_ids=true | all-gather | bytes 147456 | tf_op jit(solution)/shard_map/while/body/eval_jaxpr/all_gather | solution.py:60
  75.8 31.2 %all_gather.123 = bf16[3,512,128]{2,1,0:T(8,128)(2,1)S(1)} all-gather(bf16[3,64,128]{2,1,0:T(8,128)(2,1)} %get-tuple-element.2104), channel_id=1, replica_groups=mesh['dp'=8,'tensor'=4] {'dp'}, dimensions={1}, use_global_device_ids=true | all-gather | bytes 442368 | tf_op jit(solution)/shard_map/while/body/eval_jaxpr/all_gather | solution.py:59
  109.9 12.2 while.160
  126.0 27.9 %reduce-scatter.29.cloned.1.call-done = f32[256,512]{1,0:T(8,128)} async-done(((f32[1024,512]{1,0:T(8,128)}), f32[256,512]{1,0:T(8,128)}) %reduce-scatter.29.cloned.1.call-update) | async-done | bytes 524304 | tf_op jit(solution)/shard_map/while/body/eval_jaxpr/reduce_scatter | solution.py:116
  156.9 30.6 %all_gather.128 = bf16[128,512]{0,1:T(8,128)(2,1)S(1)} all-gather(bf16[128,64]{0,1:T(8,128)(2,1)S(1)} %copy-done.62), channel_id=1, replica_groups=mesh['dp'=8,'tensor'=4] {'dp'}, dimensions={1}, use_global_device_ids=true | all-gather | bytes 147456 | tf_op jit(solution)/shard_map/while/body/eval_jaxpr/all_gather | solution.py:63
  187.5 30.6 %all_gather.126 = bf16[512,128]{1,0:T(8,128)(2,1)S(1)} all-gather(bf16[64,128]{1,0:T(8,128)(2,1)S(1)} %copy-done.61), channel_id=1, replica_groups=mesh['dp'=8,'tensor'=4] {'dp'}, dimensions={0}, use_global_device_ids=true | all-gather | bytes 147456 | tf_op jit(solution)/shard_map/while/body/eval_jaxpr/all_gather | solution.py:61
  218.1 30.9 %all_gather.127 = bf16[2,512,128]{2,1,0:T(8,128)(2,1)S(1)} all-gather(bf16[2,64,128]{2,1,0:T(8,128)(2,1)S(1)} %copy-done.47), channel_id=1, replica_groups=mesh['dp'=8,'tensor'=4] {'dp'}, dimensions={1}, use_global_device_ids=true | all-gather | bytes 294912 | tf_op jit(solution)/shard_map/while/body/eval_jaxpr/all_gather | solution.py:62
  253.3 8.1 while.161
  265.5 30.2 %reduce-scatter.31.cloned.1.call-done = f32[256,512]{1,0:T(8,128)} async-done(((f32[1024,512]{1,0:T(8,128)}), f32[256,512]{1,0:T(8,128)}) %reduce-scatter.31.cloned.1.call-update) | async-done | bytes 524304 | tf_op jit(solution)/shard_map/while/body/eval_jaxpr/reduce_scatter | solution.py:116
  303.1 31.4 %all_gather.130 = bf16[512,512]{1,0:T(8,128)(2,1)S(1)} all-gather(bf16[64,512]{1,0:T(8,128)(2,1)S(1)} %copy-done.38), channel_id=1, replica_groups=mesh['dp'=8,'tensor'=4] {'dp'}, dimensions={0}, use_global_device_ids=true | all-gather | bytes 589824 | tf_op jit(solution)/shard_map/while/body/eval_jaxpr/all_gather | solution.py:64
  334.6 33.2 %all_gather.131 = bf16[512,512]{0,1:T(8,128)(2,1)} all-gather(bf16[512,64]{0,1:T(8,128)(2,1)S(1)} %copy-done.37), channel_id=1, replica_groups=mesh['dp'=8,'tensor'=4] {'dp'}, dimensions={1}, use_global_device_ids=true | all-gather | bytes 589824 | tf_op jit(solution)/shard_map/while/body/eval_jaxpr/all_gather | solution.py:65
  374.7 3.9 fusion.337
  381.9 31.8 %reduce-scatter.33.cloned.1.call-done = f32[256,512]{1,0:T(8,128)} async-done(((f32[1024,512]{1,0:T(8,128)}), f32[256,512]{1,0:T(8,128)}) %reduce-scatter.33.cloned.1.call-update) | async-done | bytes 524304 | tf_op jit(solution)/shard_map/while/body/eval_jaxpr/reduce_scatter | solution.py:125
  420.8 6.6 collective-permute-done.3
  431.0 2.7 collective-permute-done.5
  441.7 13.5 while.162
  456.6 2.8 fusion.340
  459.5 3.8 fusion.346
  463.4 27.3 %reduce-scatter.35.cloned.1.call-done = f32[256,512]{1,0:T(8,128)} async-done(((f32[1024,512]{1,0:T(8,128)}), f32[256,512]{1,0:T(8,128)}) %reduce-scatter.35.cloned.1.call-update) | async-done | bytes 524304 | tf_op jit(solution)/shard_map/while/body/eval_jaxpr/reduce_scatter | solution.py:363
  500.1 3.6 collective-permute-done.6
  513.3 21.8 %while.163 = (s32[]{:T(128)}, f32[1024,2,64]{0,2,1:T(8,128)S(1)}, f32[1024,2,64]{0,2,1:T(8,128)}, bf16[2,512,2,64]{1,3,2,0:T(8,128)(2,1)}, bf16[2,512,2,64]{1,3,...) while((s32[]{:T(128)}, f32[1024,2,64]{0,2,1:T(8,128)S(1)}, ...), condition=%wide.region_28.28_spmd.clone, body=%wide.region_26.27_spmd.clone.sunk | while | flops 688587264 | bytes 37259468 | solution.py:212
  526.8 3.2 fusion.384
  540.1 3.0 convolution_add_fusion.13
  543.2 4.2 convolution_add_fusion.14
  555.5 3.3 reduce-scatter.41.cloned.1.call-done
  563.0 2.9 fusion.342
  565.9 26.8 %reduce-scatter.37.cloned.1.call-done = f32[256,512]{1,0:T(8,128)} async-done(((f32[1024,512]{1,0:T(8,128)}), f32[256,512]{1,0:T(8,128)}) %reduce-scatter.37.cloned.1.call-update) | async-done | bytes 524304 | tf_op jit(solution)/shard_map/while/body/eval_jaxpr/reduce_scatter | solution.py:125
  607.3 22.2 %all-reduce.22 = (bf16[512]{0:T(512)(128)(2,1)S(1)}, bf16[512]{0:T(512)(128)(2,1)S(1)}, bf16[512]{0:T(512)(128)(2,1)S(1)}, bf16[512]{0:T(512)(128)(2,1)S(1)}, bf...) all-reduce(bf16[512]{0:T(512)(128)(2,1)S(1)} %dynamic-update-slice.18, ...), channel_id=1, replica_groups=mesh['dp'=8,'tensor'=4] {'dp'}, use_global_device_ids=true, to_apply=%add.1 | all-reduce | flops 3072 | bytes 12288 | tf_op jit(solution)/shard_map/while
  632.6 30.7 %all_gather.124 = bf16[128,512]{0,1:T(8,128)(2,1)S(1)} all-gather(bf16[128,64]{0,1:T(8,128)(2,1)} %get-tuple-element.2109), channel_id=1, replica_groups=mesh['dp'=8,'tensor'=4] {'dp'}, dimensions={1}, use_global_device_ids=true | all-gather | bytes 147456 | tf_op jit(solution)/shard_map/while/body/eval_jaxpr/all_gather | solution.py:60
  663.4 31.2 %all_gather.123 = bf16[3,512,128]{2,1,0:T(8,128)(2,1)S(1)} all-gather(bf16[3,64,128]{2,1,0:T(8,128)(2,1)} %get-tuple-element.2104), channel_id=1, replica_groups=mesh['dp'=8,'tensor'=4] {'dp'}, dimensions={1}, use_global_device_ids=true | all-gather | bytes 442368 | tf_op jit(solution)/shard_map/while/body/eval_jaxpr/all_gather | solution.py:59
  697.5 12.2 while.160
  713.5 27.0 %reduce-scatter.29.cloned.1.call-done = f32[256,512]{1,0:T(8,128)} async-done(((f32[1024,512]{1,0:T(8,128)}), f32[256,512]{1,0:T(8,128)}) %reduce-scatter.29.cloned.1.call-update) | async-done | bytes 524304 | tf_op jit(solution)/shard_map/while/body/eval_jaxpr/reduce_scatter | solution.py:116
  743.5 30.6 %all_gather.128 = bf16[128,512]{0,1:T(8,128)(2,1)S(1)} all-gather(bf16[128,64]{0,1:T(8,128)(2,1)S(1)} %copy-done.62), channel_id=1, replica_groups=mesh['dp'=8,'tensor'=4] {'dp'}, dimensions={1}, use_global_device_ids=true | all-gather | bytes 147456 | tf_op jit(solution)/shard_map/while/body/eval_jaxpr/all_gather | solution.py:63
  774.1 30.6 %all_gather.126 = bf16[512,128]{1,0:T(8,128)(2,1)S(1)} all-gather(bf16[64,128]{1,0:T(8,128)(2,1)S(1)} %copy-done.61), channel_id=1, replica_groups=mesh['dp'=8,'tensor'=4] {'dp'}, dimensions={0}, use_global_device_ids=true | all-gather | bytes 147456 | tf_op jit(solution)/shard_map/while/body/eval_jaxpr/all_gather | solution.py:61
  804.7 30.9 %all_gather.127 = bf16[2,512,128]{2,1,0:T(8,128)(2,1)S(1)} all-gather(bf16[2,64,128]{2,1,0:T(8,128)(2,1)S(1)} %copy-done.47), channel_id=1, replica_groups=mesh['dp'=8,'tensor'=4] {'dp'}, dimensions={1}, use_global_device_ids=true | all-gather | bytes 294912 | tf_op jit(solution)/shard_map/while/body/eval_jaxpr/all_gather | solution.py:62
  839.9 8.1 while.161
  852.1 30.2 %reduce-scatter.31.cloned.1.call-done = f32[256,512]{1,0:T(8,128)} async-done(((f32[1024,512]{1,0:T(8,128)}), f32[256,512]{1,0:T(8,128)}) %reduce-scatter.31.cloned.1.call-update) | async-done | bytes 524304 | tf_op jit(solution)/shard_map/while/body/eval_jaxpr/reduce_scatter | solution.py:116
  889.8 31.5 %all_gather.130 = bf16[512,512]{1,0:T(8,128)(2,1)S(1)} all-gather(bf16[64,512]{1,0:T(8,128)(2,1)S(1)} %copy-done.38), channel_id=1, replica_groups=mesh['dp'=8,'tensor'=4] {'dp'}, dimensions={0}, use_global_device_ids=true | all-gather | bytes 589824 | tf_op jit(solution)/shard_map/while/body/eval_jaxpr/all_gather | solution.py:64
  921.3 33.2 %all_gather.131 = bf16[512,512]{0,1:T(8,128)(2,1)} all-gather(bf16[512,64]{0,1:T(8,128)(2,1)S(1)} %copy-done.37), channel_id=1, replica_groups=mesh['dp'=8,'tensor'=4] {'dp'}, dimensions={1}, use_global_device_ids=true | all-gather | bytes 589824 | tf_op jit(solution)/shard_map/while/body/eval_jaxpr/all_gather | solution.py:65
  961.4 3.9 fusion.337
  968.6 31.8 %reduce-scatter.33.cloned.1.call-done = f32[256,512]{1,0:T(8,128)} async-done(((f32[1024,512]{1,0:T(8,128)}), f32[256,512]{1,0:T(8,128)}) %reduce-scatter.33.cloned.1.call-update) | async-done | bytes 524304 | tf_op jit(solution)/shard_map/while/body/eval_jaxpr/reduce_scatter | solution.py:125
  1007.5 6.6 collective-permute-done.3
  1028.7 13.5 while.162
  1043.5 2.8 fusion.340
  1046.4 3.8 fusion.346
  1050.3 27.3 %reduce-scatter.35.cloned.1.call-done = f32[256,512]{1,0:T(8,128)} async-done(((f32[1024,512]{1,0:T(8,128)}), f32[256,512]{1,0:T(8,128)}) %reduce-scatter.35.cloned.1.call-update) | async-done | bytes 524304 | tf_op jit(solution)/shard_map/while/body/eval_jaxpr/reduce_scatter | solution.py:363
  1087.0 3.6 collective-permute-done.6
  1100.2 21.8 %while.163 = (s32[]{:T(128)}, f32[1024,2,64]{0,2,1:T(8,128)S(1)}, f32[1024,2,64]{0,2,1:T(8,128)}, bf16[2,512,2,64]{1,3,2,0:T(8,128)(2,1)}, bf16[2,512,2,64]{1,3,...) while((s32[]{:T(128)}, f32[1024,2,64]{0,2,1:T(8,128)S(1)}, ...), condition=%wide.region_28.28_spmd.clone, body=%wide.region_26.27_spmd.clone.sunk | while | flops 688587264 | bytes 37259468 | solution.py:212
  1113.7 3.2 fusion.384
  1127.1 3.3 convolution_add_fusion.13
  1130.4 4.5 convolution_add_fusion.14
  1150.0 3.1 fusion.342
  1153.1 26.6 %reduce-scatter.37.cloned.1.call-done = f32[256,512]{1,0:T(8,128)} async-done(((f32[1024,512]{1,0:T(8,128)}), f32[256,512]{1,0:T(8,128)}) %reduce-scatter.37.cloned.1.call-update) | async-done | bytes 524304 | tf_op jit(solution)/shard_map/while/body/eval_jaxpr/reduce_scatter | solution.py:125
  1199.3 37.1 %all-reduce.19 = (f32[512]{0:T(512)S(1)}, f32[512]{0:T(512)S(1)}, f32[512]{0:T(512)S(1)}, f32[512]{0:T(512)S(1)}, f32[512]{0:T(512)S(1)}, /*index=5*/f32[512]{0:T(512)S(1)}) all-reduce(f32[512]{0:T(512)S(1)} %copy-done.92, f32[512]{0:T(512)S(1)} %copy-done.89, ...), channel_id=17, replica_groups=mesh['dp'=8,'tensor'=4] {'dp'}, use_global_device_ids=true, to_apply=%region_48.49.clone | all-reduce | flops 3072 | bytes 24576
  1236.8 6.4 all-reduce.20
  1243.2 9.4 reduce-scatter.19.cloned.1.call-done
  1252.7 64.1 %reduce-scatter.17.cloned.1.call-done = f32[128,64]{0,1:T(8,128)} async-done(((f32[128,512]{0,1:T(8,128)}), f32[128,64]{0,1:T(8,128)}) %reduce-scatter.17.cloned.1.call-update) | async-done | bytes 32784 | tf_op jit(solution)/shard_map/reduce_scatter | solution.py:92
  1316.8 64.2 %reduce-scatter.23.cloned.1.call-done = f32[128,64]{0,1:T(8,128)} async-done(((f32[128,512]{0,1:T(8,128)}), f32[128,64]{0,1:T(8,128)}) %reduce-scatter.23.cloned.1.call-update) | async-done | bytes 32784 | tf_op jit(solution)/shard_map/reduce_scatter | solution.py:95
  1381.0 65.1 %reduce-scatter.21.cloned.1.call-done = f32[2,64,128]{2,1,0:T(8,128)} async-done(((f32[2,512,128]{2,1,0:T(8,128)}), f32[2,64,128]{2,1,0:T(8,128)}) %reduce-scatter.21.cloned.1.call-update) | async-done | bytes 65552 | tf_op jit(solution)/shard_map/reduce_scatter | solution.py:94
  1446.1 66.5 %reduce-scatter.15.cloned.1.call-done = f32[3,64,128]{2,1,0:T(8,128)} async-done(((f32[3,512,128]{2,1,0:T(8,128)}), f32[3,64,128]{2,1,0:T(8,128)}) %reduce-scatter.15.cloned.1.call-update) | async-done | bytes 98320 | tf_op jit(solution)/shard_map/reduce_scatter | solution.py:91
  1512.6 66.5 %reduce-scatter.25.cloned.1.call-done = f32[64,512]{1,0:T(8,128)} async-done(((f32[512,512]{1,0:T(8,128)}), f32[64,512]{1,0:T(8,128)}) %reduce-scatter.25.cloned.1.call-update) | async-done | bytes 131088 | tf_op jit(solution)/shard_map/reduce_scatter | solution.py:96
  1579.1 66.8 %reduce-scatter.27.cloned.1.call-done = f32[512,64]{0,1:T(8,128)} async-done(((f32[512,512]{0,1:T(8,128)}), f32[512,64]{0,1:T(8,128)}) %reduce-scatter.27.cloned.1.call-update) | async-done | bytes 131088 | tf_op jit(solution)/shard_map/reduce_scatter | solution.py:97
  (890 shorter events, 332.3 us)
Async XLA Ops:
  8.6 98.4 %all-gather.9.cloned.1.call-start = ((), (), s32[]{:S(2)}) async-start(), calls=%async_computation.21 | async-start | bytes 1310720 | tf_op jit(solution)/shard_map/while/body/eval_jaxpr/all_gather | solution.py:108
  9.8 66.0 %copy-start.42 = (f32[256]{0:T(256)}, f32[256]{0:T(256)S(1)}, u32[]{:S(2)}) copy-start(f32[256]{0:T(256)S(1)} %broadcast_multiply_fusion.6) | copy-start | bytes 3076 | tf_op jit(solution)/shard_map/while
  11.0 64.8 %copy-start.55 = (f32[256]{0:T(256)}, f32[256]{0:T(256)S(1)}, u32[]{:S(2)}) copy-start(f32[256]{0:T(256)S(1)} %fusion.324) | copy-start | bytes 3076 | tf_op jit(solution)/shard_map/while
  43.8 110.1 %reduce-scatter.29.cloned.1.call-start = ((), (), s32[]{:S(2)}) async-start(), calls=%async_computation.22 | async-start | bytes 2621440 | tf_op jit(solution)/shard_map/while/body/eval_jaxpr/reduce_scatter | solution.py:116
  123.2 64.3 %copy-start.61 = (bf16[64,128]{1,0:T(8,128)(2,1)S(1)}, bf16[64,128]{1,0:T(8,128)(2,1)}, u32[]{:S(2)}) copy-start(bf16[64,128]{1,0:T(8,128)(2,1)} %get-tuple-element.2112) | copy-start | bytes 49156 | tf_op jit(solution)/shard_map/while
  123.2 94.9 %copy-start.47 = (bf16[2,64,128]{2,1,0:T(8,128)(2,1)S(1)}, bf16[2,64,128]{2,1,0:T(8,128)(2,1)}, u32[]{:S(2)}) copy-start(bf16[2,64,128]{2,1,0:T(8,128)(2,1)} %get-tuple-element.2114) | copy-start | bytes 98308 | tf_op jit(solution)/shard_map/while
  125.1 123.9 %all-gather.13.cloned.1.call-start = ((), (), s32[]{:S(2)}) async-start(), calls=%async_computation.24 | async-start | bytes 1310720 | tf_op jit(solution)/shard_map/while/body/eval_jaxpr/all_gather | solution.py:300
  125.9 125.0 %all-gather.11.cloned.1.call-start = ((), (), s32[]{:S(2)}) async-start(), calls=%async_computation.23 | async-start | bytes 1310720 | tf_op jit(solution)/shard_map/while/body/eval_jaxpr/all_gather | solution.py:299
  125.9 123.1 %copy-start.44 = (f32[512]{0:T(512)}, f32[512]{0:T(512)S(1)}, u32[]{:S(2)}) copy-start(f32[512]{0:T(512)S(1)} %convert_element_type.393) | copy-start | bytes 6148 | tf_op jit(solution)/shard_map/while
  155.1 98.1 %copy-start.48 = (f32[256]{0:T(256)}, f32[256]{0:T(256)S(1)}, u32[]{:S(2)}) copy-start(f32[256]{0:T(256)S(1)} %broadcast_multiply_fusion.7) | copy-start | bytes 3076 | tf_op jit(solution)/shard_map/while
  155.3 97.9 %copy-start.65 = (f32[256]{0:T(256)}, f32[256]{0:T(256)S(1)}, u32[]{:S(2)}) copy-start(f32[256]{0:T(256)S(1)} %multiply_reduce_fusion.14) | copy-start | bytes 3076 | tf_op jit(solution)/shard_map/while
  155.3 97.9 %copy-start.57 = (f32[256]{0:T(256)}, f32[256]{0:T(256)S(1)}, u32[]{:S(2)}) copy-start(f32[256]{0:T(256)S(1)} %fusion.330) | copy-start | bytes 3076 | tf_op jit(solution)/shard_map/while
  156.3 139.4 %reduce-scatter.31.cloned.1.call-start = ((), (), s32[]{:S(2)}) async-start(), calls=%async_computation.25 | async-start | bytes 2621440 | tf_op jit(solution)/shard_map/while/body/eval_jaxpr/reduce_scatter | solution.py:116
  264.2 70.4 %copy-start.37 = (bf16[512,64]{0,1:T(8,128)(2,1)S(1)}, bf16[512,64]{0,1:T(8,128)(2,1)}, u32[]{:S(2)}) copy-start(bf16[512,64]{0,1:T(8,128)(2,1)} %get-tuple-element.2108) | copy-start | bytes 196612 | tf_op jit(solution)/shard_map/while
  264.2 108.6 %all-gather.15.cloned.1.call-start = ((), (), s32[]{:S(2)}) async-start(), calls=%async_computation.26 | async-start | bytes 1310720 | tf_op jit(solution)/shard_map/while/body/eval_jaxpr/all_gather | solution.py:108
  299.7 113.9 %reduce-scatter.33.cloned.1.call-start = ((), (), s32[]{:S(2)}) async-start(), calls=%async_computation.27 | async-start | bytes 2621440 | tf_op jit(solution)/shard_map/while/body/eval_jaxpr/reduce_scatter | solution.py:125
  301.4 33.2 %collective-permute-start = (bf16[256,512]{1,0:T(8,128)(2,1)}, bf16[256,512]{1,0:T(8,128)(2,1)}, u32[]{:S(2)}, u32[]{:S(2)}) collective-permute-start(bf16[256,512]{1,0:T(8,128)(2,1)} %get-tuple-element.1760), channel_id=1, source_target_pairs={{0,1},{1,2},{2,3},{3,0},{4,5},{5,6},{6,7},{7,4},{8,9},{9,10},{10,1... | collective-permute-start | bytes 786440 | tf_op jit(solution)/shard_map/while/body/eval_jaxpr/ppermute | solution.py:21
  301.4 68.1 %collective-permute-start.1 = (bf16[256,512]{1,0:T(8,128)(2,1)}, bf16[256,512]{1,0:T(8,128)(2,1)}, u32[]{:S(2)}, u32[]{:S(2)}) collective-permute-start(bf16[256,512]{1,0:T(8,128)(2,1)} %get-tuple-element.1760), channel_id=1, source_target_pairs={{0,3},{1,0},{2,1},{3,2},{4,7},{5,4},{6,5},{7,6},{8,11},{9,8},{10,9... | collective-permute-start | bytes 786440 | tf_op jit(solution)/shard_map/while/body/eval_jaxpr/ppermute | solution.py:26
  334.5 36.6 %collective-permute-start.2 = (bf16[256,512]{1,0:T(8,128)(2,1)}, bf16[256,512]{1,0:T(8,128)(2,1)}, u32[]{:S(2)}, u32[]{:S(2)}) collective-permute-start(bf16[256,512]{1,0:T(8,128)(2,1)} %collective-permute-done), channel_id=1, source_target_pairs={{0,1},{1,2},{2,3},{3,0},{4,5},{5,6},{6,7},{7,4},{8,9},{9,10},{10,1... | collective-permute-start | bytes 786440 | tf_op jit(solution)/shard_map/while/body/eval_jaxpr/ppermute | solution.py:21
  381.8 108.9 %reduce-scatter.35.cloned.1.call-start = ((), (), s32[]{:S(2)}) async-start(), calls=%async_computation.28 | async-start | bytes 2621440 | tf_op jit(solution)/shard_map/while/body/eval_jaxpr/reduce_scatter | solution.py:363
  419.0 8.4 collective-permute-start.3
  419.0 10.3 collective-permute-start.4
  427.4 6.3 collective-permute-start.5
  459.4 88.1 %reduce-scatter.39.cloned.1.call-start = ((), (), s32[]{:S(2)}) async-start(), calls=%async_computation.30 | async-start | bytes 2621440 | tf_op jit(solution)/shard_map/while/body/eval_jaxpr/reduce_scatter | solution.py:116
  463.3 95.4 %reduce-scatter.41.cloned.1.call-start = ((), (), s32[]{:S(2)}) async-start(), calls=%async_computation.31 | async-start | bytes 2621440 | tf_op jit(solution)/shard_map/while/body/eval_jaxpr/reduce_scatter | solution.py:364
  497.1 6.6 collective-permute-start.6
  498.3 8.5 collective-permute-start.7
  503.7 5.8 collective-permute-start.8
  505.6 87.1 %reduce-scatter.37.cloned.1.call-start = ((), (), s32[]{:S(2)}) async-start(), calls=%async_computation.29 | async-start | bytes 2621440 | tf_op jit(solution)/shard_map/while/body/eval_jaxpr/reduce_scatter | solution.py:125
  597.9 96.6 %all-gather.9.cloned.1.call-start = ((), (), s32[]{:S(2)}) async-start(), calls=%async_computation.21 | async-start | bytes 1310720 | tf_op jit(solution)/shard_map/while/body/eval_jaxpr/all_gather | solution.py:108
  599.1 64.3 %copy-start.42 = (f32[256]{0:T(256)}, f32[256]{0:T(256)S(1)}, u32[]{:S(2)}) copy-start(f32[256]{0:T(256)S(1)} %broadcast_multiply_fusion.6) | copy-start | bytes 3076 | tf_op jit(solution)/shard_map/while
  631.3 109.1 %reduce-scatter.29.cloned.1.call-start = ((), (), s32[]{:S(2)}) async-start(), calls=%async_computation.22 | async-start | bytes 2621440 | tf_op jit(solution)/shard_map/while/body/eval_jaxpr/reduce_scatter | solution.py:116
  710.8 63.3 %copy-start.61 = (bf16[64,128]{1,0:T(8,128)(2,1)S(1)}, bf16[64,128]{1,0:T(8,128)(2,1)}, u32[]{:S(2)}) copy-start(bf16[64,128]{1,0:T(8,128)(2,1)} %get-tuple-element.2112) | copy-start | bytes 49156 | tf_op jit(solution)/shard_map/while
  710.8 93.9 %copy-start.47 = (bf16[2,64,128]{2,1,0:T(8,128)(2,1)S(1)}, bf16[2,64,128]{2,1,0:T(8,128)(2,1)}, u32[]{:S(2)}) copy-start(bf16[2,64,128]{2,1,0:T(8,128)(2,1)} %get-tuple-element.2114) | copy-start | bytes 98308 | tf_op jit(solution)/shard_map/while
  712.6 123.0 %all-gather.13.cloned.1.call-start = ((), (), s32[]{:S(2)}) async-start(), calls=%async_computation.24 | async-start | bytes 1310720 | tf_op jit(solution)/shard_map/while/body/eval_jaxpr/all_gather | solution.py:300
  713.4 124.1 %all-gather.11.cloned.1.call-start = ((), (), s32[]{:S(2)}) async-start(), calls=%async_computation.23 | async-start | bytes 1310720 | tf_op jit(solution)/shard_map/while/body/eval_jaxpr/all_gather | solution.py:299
  713.5 122.1 %copy-start.44 = (f32[512]{0:T(512)}, f32[512]{0:T(512)S(1)}, u32[]{:S(2)}) copy-start(f32[512]{0:T(512)S(1)} %convert_element_type.393) | copy-start | bytes 6148 | tf_op jit(solution)/shard_map/while
  741.7 98.2 %copy-start.48 = (f32[256]{0:T(256)}, f32[256]{0:T(256)S(1)}, u32[]{:S(2)}) copy-start(f32[256]{0:T(256)S(1)} %broadcast_multiply_fusion.7) | copy-start | bytes 3076 | tf_op jit(solution)/shard_map/while
  741.9 98.0 %copy-start.65 = (f32[256]{0:T(256)}, f32[256]{0:T(256)S(1)}, u32[]{:S(2)}) copy-start(f32[256]{0:T(256)S(1)} %multiply_reduce_fusion.14) | copy-start | bytes 3076 | tf_op jit(solution)/shard_map/while
  741.9 98.0 %copy-start.57 = (f32[256]{0:T(256)}, f32[256]{0:T(256)S(1)}, u32[]{:S(2)}) copy-start(f32[256]{0:T(256)S(1)} %fusion.330) | copy-start | bytes 3076 | tf_op jit(solution)/shard_map/while
  742.8 139.4 %reduce-scatter.31.cloned.1.call-start = ((), (), s32[]{:S(2)}) async-start(), calls=%async_computation.25 | async-start | bytes 2621440 | tf_op jit(solution)/shard_map/while/body/eval_jaxpr/reduce_scatter | solution.py:116
  850.8 70.5 %copy-start.37 = (bf16[512,64]{0,1:T(8,128)(2,1)S(1)}, bf16[512,64]{0,1:T(8,128)(2,1)}, u32[]{:S(2)}) copy-start(bf16[512,64]{0,1:T(8,128)(2,1)} %get-tuple-element.2108) | copy-start | bytes 196612 | tf_op jit(solution)/shard_map/while
  850.9 108.6 %all-gather.15.cloned.1.call-start = ((), (), s32[]{:S(2)}) async-start(), calls=%async_computation.26 | async-start | bytes 1310720 | tf_op jit(solution)/shard_map/while/body/eval_jaxpr/all_gather | solution.py:108
  886.4 114.0 %reduce-scatter.33.cloned.1.call-start = ((), (), s32[]{:S(2)}) async-start(), calls=%async_computation.27 | async-start | bytes 2621440 | tf_op jit(solution)/shard_map/while/body/eval_jaxpr/reduce_scatter | solution.py:125
  888.0 33.2 %collective-permute-start = (bf16[256,512]{1,0:T(8,128)(2,1)}, bf16[256,512]{1,0:T(8,128)(2,1)}, u32[]{:S(2)}, u32[]{:S(2)}) collective-permute-start(bf16[256,512]{1,0:T(8,128)(2,1)} %get-tuple-element.1760), channel_id=1, source_target_pairs={{0,1},{1,2},{2,3},{3,0},{4,5},{5,6},{6,7},{7,4},{8,9},{9,10},{10,1... | collective-permute-start | bytes 786440 | tf_op jit(solution)/shard_map/while/body/eval_jaxpr/ppermute | solution.py:21
  888.0 68.1 %collective-permute-start.1 = (bf16[256,512]{1,0:T(8,128)(2,1)}, bf16[256,512]{1,0:T(8,128)(2,1)}, u32[]{:S(2)}, u32[]{:S(2)}) collective-permute-start(bf16[256,512]{1,0:T(8,128)(2,1)} %get-tuple-element.1760), channel_id=1, source_target_pairs={{0,3},{1,0},{2,1},{3,2},{4,7},{5,4},{6,5},{7,6},{8,11},{9,8},{10,9... | collective-permute-start | bytes 786440 | tf_op jit(solution)/shard_map/while/body/eval_jaxpr/ppermute | solution.py:26
  921.3 36.6 %collective-permute-start.2 = (bf16[256,512]{1,0:T(8,128)(2,1)}, bf16[256,512]{1,0:T(8,128)(2,1)}, u32[]{:S(2)}, u32[]{:S(2)}) collective-permute-start(bf16[256,512]{1,0:T(8,128)(2,1)} %collective-permute-done), channel_id=1, source_target_pairs={{0,1},{1,2},{2,3},{3,0},{4,5},{5,6},{6,7},{7,4},{8,9},{9,10},{10,1... | collective-permute-start | bytes 786440 | tf_op jit(solution)/shard_map/while/body/eval_jaxpr/ppermute | solution.py:21
  968.5 109.1 %reduce-scatter.35.cloned.1.call-start = ((), (), s32[]{:S(2)}) async-start(), calls=%async_computation.28 | async-start | bytes 2621440 | tf_op jit(solution)/shard_map/while/body/eval_jaxpr/reduce_scatter | solution.py:363
  1005.8 8.4 collective-permute-start.3
  1005.8 10.5 collective-permute-start.4
  1014.1 6.5 collective-permute-start.5
  1046.4 88.7 %reduce-scatter.39.cloned.1.call-start = ((), (), s32[]{:S(2)}) async-start(), calls=%async_computation.30 | async-start | bytes 2621440 | tf_op jit(solution)/shard_map/while/body/eval_jaxpr/reduce_scatter | solution.py:116
  1050.3 95.4 %reduce-scatter.41.cloned.1.call-start = ((), (), s32[]{:S(2)}) async-start(), calls=%async_computation.31 | async-start | bytes 2621440 | tf_op jit(solution)/shard_map/while/body/eval_jaxpr/reduce_scatter | solution.py:364
  1084.0 6.6 collective-permute-start.6
  1085.2 8.2 collective-permute-start.7
  1090.6 5.8 collective-permute-start.8
  1092.5 87.2 %reduce-scatter.37.cloned.1.call-start = ((), (), s32[]{:S(2)}) async-start(), calls=%async_computation.29 | async-start | bytes 2621440 | tf_op jit(solution)/shard_map/while/body/eval_jaxpr/reduce_scatter | solution.py:125
  1186.9 65.8 %reduce-scatter.19.cloned.1.call-start = ((), (), s32[]{:S(2)}) async-start(), calls=%async_computation.16 | async-start | bytes 294912 | tf_op jit(solution)/shard_map/reduce_scatter | solution.py:93
  1187.5 129.3 %reduce-scatter.17.cloned.1.call-start = ((), (), s32[]{:S(2)}) async-start(), calls=%async_computation.15 | async-start | bytes 294912 | tf_op jit(solution)/shard_map/reduce_scatter | solution.py:92
  1189.4 191.6 %reduce-scatter.23.cloned.1.call-start = ((), (), s32[]{:S(2)}) async-start(), calls=%async_computation.18 | async-start | bytes 294912 | tf_op jit(solution)/shard_map/reduce_scatter | solution.py:95
  1191.3 254.8 %reduce-scatter.21.cloned.1.call-start = ((), (), s32[]{:S(2)}) async-start(), calls=%async_computation.17 | async-start | bytes 589824 | tf_op jit(solution)/shard_map/reduce_scatter | solution.py:94
  1193.4 319.2 %reduce-scatter.15.cloned.1.call-start = ((), (), s32[]{:S(2)}) async-start(), calls=%async_computation.14 | async-start | bytes 884736 | tf_op jit(solution)/shard_map/reduce_scatter | solution.py:91
  1195.8 383.4 %reduce-scatter.25.cloned.1.call-start = ((), (), s32[]{:S(2)}) async-start(), calls=%async_computation.19 | async-start | bytes 1179648 | tf_op jit(solution)/shard_map/reduce_scatter | solution.py:96
  1196.5 449.4 %reduce-scatter.27.cloned.1.call-start = ((), (), s32[]{:S(2)}) async-start(), calls=%async_computation.20 | async-start | bytes 1179648 | tf_op jit(solution)/shard_map/reduce_scatter | solution.py:97
  (181 other events, 3039.4 us)
Sparse Core Ops, SparseCore 0:
  43.9 13.9 all-gather.8
  125.2 28.6 reduce-scatter.28
  155.5 16.7 all-gather.12
  173.8 16.7 all-gather.10
  264.4 31.2 reduce-scatter.30
  299.9 17.3 all-gather.14
  381.9 31.6 reduce-scatter.32
  459.5 31.1 reduce-scatter.34
  493.3 31.4 reduce-scatter.38
  527.3 31.3 reduce-scatter.40
  561.3 31.4 reduce-scatter.36
  631.5 13.0 all-gather.8
  712.7 27.7 reduce-scatter.28
  742.0 16.7 all-gather.12
  760.2 16.7 all-gather.10
  851.0 31.2 reduce-scatter.30
  886.5 17.3 all-gather.14
  968.6 31.7 reduce-scatter.32
  1046.4 31.1 reduce-scatter.34
  1080.0 31.4 reduce-scatter.38
  1114.2 31.4 reduce-scatter.40
  1148.2 31.4 reduce-scatter.36
Sparse Core Ops, SparseCore 1:
  1191.3 61.3 reduce-scatter.18
  1256.4 60.3 reduce-scatter.16
  1320.6 60.3 reduce-scatter.22
  1384.9 61.1 reduce-scatter.20
  1450.4 62.2 reduce-scatter.14
  1516.6 62.5 reduce-scatter.24
  1583.4 62.5 reduce-scatter.26
